TPU v7x, 256 devices: a whole 4x4x8 slice. The times are simulated.
256 devices in a mesh: head: 8 (over x_hi, y), key: 8 (over z), hid: 4 (over x_lo, core).
Axes of the slice: x: 4 (x_hi: 2, x_lo: 2; x = x_hi * 2 + x_lo), y: 4, z: 8, core: 2. Of those that a mesh axis runs over, the one named last changes fastest.
Arguments:
- tokens: bfloat16 [2048, 8192], P('key', 'hid'), may hold values from -6 to 6
- query_weight: bfloat16 [8192, 8192], P('hid', 'head'), may hold values from -0.0625 to 0.0625
- key_weight: bfloat16 [8192, 1024], P('hid', 'head'), may hold values from -0.0625 to 0.0625
- value_weight: bfloat16 [8192, 1024], P('hid', 'head'), may hold values from -0.0625 to 0.0625
- output_weight: bfloat16 [8192, 8192], P(('head', 'hid')), may hold values from -0.125 to 0.125
- key_cache: bfloat16 [16384, 8, 128], P('key', 'head'), may hold values from -2000 to 2000
- value_cache: bfloat16 [16384, 8, 128], P('key', 'head'), may hold values from -6 to 6
- cache_places: int32 [64], P('key'), may hold values from 1 to 510, as said below
- slab_places: int32 [8], replicated, may hold values from 0 to 511, as said below
Outputs:
- attended: bfloat16 [2048, 8192], P('key', ('head', 'hid'))
Inputs may be any that keep to these rules, and one draw needn't show every extreme that they name: The 64 entries of cache_places and the 8 entries of slab_places are all different from one another. `slab_places`: see cache_places: no slab shares a block number with another slab or with a resident block.
All inputs are finite; a program needn't handle non-finite values.
Results may differ from a plain program's by a relative error of at most 0.039.
Values may be sent and summed in bfloat16 or wider, within the bound.
No kernel may reach another device: no remote copies, remote signals or barrier semaphores. Data moves between devices by JAX's collectives and lax.ppermute only.
A program may use at most 128 MiB of HBM per device.

v0:
```python
import functools
import math

import jax
import jax.numpy as jnp
import numpy as np
from jax import lax
from jax.experimental import pallas as pl
from jax.experimental.pallas import tpu as pltpu
from jax.sharding import Mesh
from jax.sharding import PartitionSpec as P

HID = ("hid_0", "hid_1")
HEAD = ("head_0", "head_1")
HEAD_HID = ("head_0", "head_1", "hid_0", "hid_1")
ALONG_X = ("head_0", "hid_0")

THETA = 500000.0
NEGATIVE = -1e30
BF16 = jnp.bfloat16
F32 = jnp.float32

ROWS = 256
HD = 128
PAIR = 2 * HD
NEW = 64
QUARTER = 512
HALF = ROWS + 16
LOAD = 4 * HALF
MSG = ROWS + 16
TALL = 2048
EXPONENT = math.log2(math.e) / math.sqrt(HD)
CONTRACT = (((1,), (1,)), ((), ()))

VMEM = pl.BlockSpec(memory_space=pltpu.VMEM)
SMEM = pl.BlockSpec(memory_space=pltpu.SMEM)
HBM = pl.BlockSpec(memory_space=pltpu.HBM)


def shaped(shape, dtype):
    return jax.ShapeDtypeStruct(shape, dtype)


def params(mib=60):
    return pltpu.CompilerParams(vmem_limit_bytes=mib * 2**20)


SMALL = pl.CostEstimate(flops=1, bytes_accessed=1, transcendentals=0)
MEDIUM = pl.CostEstimate(flops=2**27, bytes_accessed=2**18, transcendentals=2**10)


def shift(n, by):
    return [(i, (i + by) % n) for i in range(n)]


def swap(array, axis):
    return lax.ppermute(array, axis, shift(2, 1))


def hid_index():
    return 2 * lax.axis_index("hid_0") + lax.axis_index("hid_1")


def fetch(pairs, sems):
    copies = [
        pltpu.make_async_copy(source, target, sems.at[i])
        for i, (source, target) in enumerate(pairs)
    ]
    for copy in copies:
        copy.start()
    return copies


def pack_kernel(places, slabs, keys, values, out, spots, load, sems):
    core = lax.axis_index("hid_1")
    lane = lax.broadcasted_iota(jnp.int32, (16, PAIR), 1)
    pairs = []
    for i in range(4):
        block = 4 * lax.axis_index("hid_0") + lax.rem(2 * core + i, 4)
        rows = pl.ds(pl.multiple_of(block * ROWS, ROWS), ROWS)
        to = slice(i * HALF, i * HALF + ROWS)
        pairs.append((keys.at[rows, :], load.at[to, :HD]))
        pairs.append((values.at[rows, :], load.at[to, HD:]))
        place = places[block]
        table = jnp.where(lane == 0, place >> 1, jnp.where(lane == 1, place & 1, 0))
        load[i * HALF + ROWS : (i + 1) * HALF, :] = table.astype(F32).astype(BF16)
    copies = fetch(pairs, sems.at[:8])
    leaving = []
    for i in range(4):
        copies[2 * i].wait()
        copies[2 * i + 1].wait()
        to = slice(i * HALF, (i + 1) * HALF)
        leaving += fetch([(load.at[to, :], out.at[to, :])], sems.at[8 + i : 9 + i])
    row = lax.broadcasted_iota(jnp.int32, (ROWS, HD), 0)
    spots[...] = (slabs[lax.axis_index("key")] * ROWS + row).astype(F32)
    for copy in leaving:
        copy.wait()


def pack(places, slabs, keys, values):
    return pl.pallas_call(
        pack_kernel,
        out_shape=[shaped((LOAD, PAIR), BF16), shaped((ROWS, HD), F32)],
        in_specs=[SMEM, SMEM, HBM, HBM],
        out_specs=[HBM, VMEM],
        scratch_shapes=[pltpu.VMEM((LOAD, PAIR), BF16), pltpu.SemaphoreType.DMA((12,))],
        compiler_params=params(),
        cost_estimate=SMALL,
        name="pack",
    )(places, slabs, keys, values)


def columns_kernel(weight, *refs):
    outs, pieces, sems, out_sems = refs[:4], refs[4], refs[5], refs[6]
    y = lax.axis_index("head_1")
    pairs = []
    for t, by in enumerate((2, 1, 3, 0)):
        at = lax.rem(y + by, 4) * 1024
        for hi in range(2):
            source = pl.ds(pl.multiple_of(hi * 4096 + at, 1024), 1024)
            pairs.append((weight.at[:, source], pieces.at[t, :, hi * 1024 : (hi + 1) * 1024]))
    copies = fetch(pairs, sems)
    leaving = []
    for t in range(4):
        copies[2 * t].wait()
        copies[2 * t + 1].wait()
        leaving += fetch([(pieces.at[t], outs[t])], out_sems.at[t : t + 1])
    for copy in leaving:
        copy.wait()


def columns(weight):
    return pl.pallas_call(
        columns_kernel,
        out_shape=[shaped((ROWS, 2048), BF16)] * 4,
        in_specs=[HBM],
        out_specs=[HBM] * 4,
        scratch_shapes=[
            pltpu.VMEM((4, ROWS, 2048), BF16),
            pltpu.SemaphoreType.DMA((8,)),
            pltpu.SemaphoreType.DMA((4,)),
        ],
        compiler_params=params(),
        cost_estimate=SMALL,
        name="columns",
    )(weight)


def first_kernel(tokens, query, key, value, send, keep, tok, wide, kv, sent, fresh, sems):
    core = lax.axis_index("hid_1")
    deep = tok.shape[2]
    copies = []
    for t in range(4):
        part = slice(t * deep, (t + 1) * deep)
        pairs = [
            (tokens.at[:, part], tok.at[t]),
            (query.at[part, :], wide.at[t]),
            (key.at[part, :], kv.at[t, :, :HD]),
            (value.at[part, :], kv.at[t, :, HD:]),
        ]
        copies.append(fetch(pairs, sems.at[4 * t : 4 * t + 4]))
    far_cols = pl.ds(pl.multiple_of((1 - core) * 512, 512), 512)
    near_cols = pl.ds(pl.multiple_of(core * 512, 512), 512)
    for t in range(4):
        for copy in copies[t]:
            copy.wait()
        a = tok[t]
        far = jnp.dot(a, wide[t, :, far_cols], preferred_element_type=F32)
        near = jnp.dot(a, wide[t, :, near_cols], preferred_element_type=F32)
        new = jnp.dot(a, kv[t], preferred_element_type=F32)
        if t == 0:
            sent[...] = far
            keep[:ROWS, :] = near
            fresh[...] = new
        else:
            keep[:ROWS, :] += near
            fresh[...] += new
            if t == 3:
                send[:ROWS, :] = (sent[...] + far).astype(BF16)
            else:
                sent[...] += far
    for t in range(2):
        cols = slice(t * PAIR, (t + 1) * PAIR)
        far_rows = pl.ds(pl.multiple_of((1 - core) * 128 + t * NEW, NEW), NEW)
        near_rows = pl.ds(pl.multiple_of(core * 128 + t * NEW, NEW), NEW)
        send[ROWS:, cols] = fresh[far_rows, :].astype(BF16)
        keep[ROWS:, cols] = fresh[near_rows, :]


def first(tokens, query, key, value):
    deep = tokens.shape[1] // 4
    return pl.pallas_call(
        first_kernel,
        out_shape=[shaped((320, 512), BF16), shaped((320, 512), F32)],
        in_specs=[HBM] * 4,
        out_specs=[VMEM] * 2,
        scratch_shapes=[
            pltpu.VMEM((4, ROWS, deep), BF16),
            pltpu.VMEM((4, deep, query.shape[1]), BF16),
            pltpu.VMEM((4, deep, PAIR), BF16),
            pltpu.VMEM((ROWS, 512), F32),
            pltpu.VMEM((ROWS, PAIR), F32),
            pltpu.SemaphoreType.DMA((16,)),
        ],
        compiler_params=params(),
        cost_estimate=SMALL,
        name="first",
    )(tokens, query, key, value)


def second_kernel(keep, got, send, onward):
    x = lax.axis_index("hid_0")
    q = keep[:ROWS, :] + got[:ROWS, :].astype(F32)
    send[:ROWS, :] = q.astype(BF16)
    onward[:ROWS, :] = q
    low = keep[ROWS:, :] + got[ROWS:, :].astype(F32)
    sides = [low[:, :PAIR], low[:, PAIR:]]
    sides = [jnp.concatenate([s[:32], s[32:]], axis=1) for s in sides]
    mine = jnp.where(x == 0, sides[0], sides[1])
    other = jnp.where(x == 0, sides[1], sides[0])
    send[ROWS:, :] = other.astype(BF16)
    onward[ROWS:, :] = mine


def second(keep, got):
    return pl.pallas_call(
        second_kernel,
        out_shape=[shaped((288, 512), BF16), shaped((288, 512), F32)],
        in_specs=[VMEM] * 2,
        out_specs=[VMEM] * 2,
        compiler_params=params(8),
        cost_estimate=SMALL,
        name="second",
    )(keep, got)


def new_offset():
    return lax.axis_index("hid_1") * 128 + lax.axis_index("hid_0") * NEW


def rotate_kernel(keep, got, cosine, sine, queries, notes):
    for h in range(4):
        cols = slice(h * HD, (h + 1) * HD)
        u = keep[:ROWS, cols] + got[:ROWS, cols].astype(F32)
        turned = u * cosine[...] + pltpu.roll(u, HD // 2, 1) * sine[...]
        queries[:, cols] = turned.astype(BF16)
    low = keep[ROWS:, :] + got[ROWS:, :].astype(F32)
    low = jnp.concatenate([low[:, :PAIR], low[:, PAIR:]], axis=0)
    rows = pl.ds(pl.multiple_of(new_offset(), NEW), NEW)
    u = low[:, :HD]
    turned = u * cosine[rows, :] + pltpu.roll(u, HD // 2, 1) * sine[rows, :]
    for z in range(8):
        notes[z, :, :HD] = turned.astype(BF16)
        notes[z, :, HD:] = low[:, HD:].astype(BF16)


def rotated(keep, got, cosine, sine):
    return pl.pallas_call(
        rotate_kernel,
        out_shape=[shaped((ROWS, 512), BF16), shaped((8, NEW, PAIR), BF16)],
        in_specs=[VMEM] * 4,
        out_specs=[VMEM] * 2,
        compiler_params=params(8),
        cost_estimate=SMALL,
        name="rotated",
    )(keep, got, cosine, sine)


def gather_visible(mine, slabs, halves, new, keys, values, chunk):
    height = keys.shape[0]
    values[:, HD:] = jnp.ones((height, HD), BF16)
    n = jnp.int32(0)
    lane = lax.broadcasted_iota(jnp.int32, (16, HD), 1)
    marks = jnp.zeros((16, HD), jnp.int32)
    for i, load in enumerate(halves):
        codes = load[ROWS:, :HD].astype(F32)
        codes = jnp.where(lane == 0, 2.0, 1.0) * codes
        place = (codes + pltpu.roll(codes, HD - 1, 1)).astype(jnp.int32)
        marks = marks + jnp.where(place < mine, 1 << i, 0)
    mask = jnp.max(jnp.where(lane == 0, marks, 0))
    bit = 0
    for load in halves:
        seen = ((mask >> bit) & 1) == 1
        bit += 1

        @pl.when(seen)
        def _(load=load, n=n):
            at = pl.ds(pl.multiple_of(n * NEW, NEW), ROWS)
            keys[at, :] = load[:ROWS, :HD]
            values[at, :HD] = load[:ROWS, HD:]

        n = n + jnp.where(seen, ROWS // NEW, 0)
    if new is not None:
        for z in range(8):
            seen = slabs[z] < mine

            @pl.when(seen)
            def _(z=z, n=n):
                at = pl.ds(pl.multiple_of(n * NEW, NEW), NEW)
                keys[at, :] = new[z, :, :HD]
                values[at, :HD] = new[z, :, HD:]

            n = n + jnp.where(seen, 1, 0)
    per = chunk // NEW
    chunks = (n + per - 1) // per

    def pad(t, carry):
        at = pl.ds(pl.multiple_of(t * NEW, NEW), NEW)
        keys[at, :] = keys[:NEW, :]
        values[at, :] = jnp.zeros((NEW, PAIR), BF16)
        return carry

    lax.fori_loop(n, chunks * per, pad, 0)
    return chunks


def attend(q, peak_ref, chunks, keys, values, scores, chunk, acc_at, before):
    def peaks(i, carry):
        at = pl.ds(pl.multiple_of(i * chunk, chunk), chunk)
        s = lax.dot_general(q, keys[at, :], CONTRACT, preferred_element_type=F32)
        scores[i] = s
        best = peak_ref[...]
        for t in range(chunk // HD):
            best = jnp.maximum(best, s[:, t * HD : (t + 1) * HD])
        peak_ref[...] = best
        return carry

    lax.fori_loop(0, chunks, peaks, 0)
    peak = jnp.max(peak_ref[...], axis=1, keepdims=True)
    acc_at[...] = before(peak)

    def weigh(i, carry):
        at = pl.ds(pl.multiple_of(i * chunk, chunk), chunk)
        p = jnp.exp2((scores[i] - peak) * EXPONENT).astype(BF16)
        acc_at[...] += jnp.dot(p, values[at, :], preferred_element_type=F32)
        return carry

    lax.fori_loop(0, chunks, weigh, 0)
    return peak


def halves_of(buffers):
    halves = []
    for ref in buffers:
        for b in range(ref.shape[0] // HALF):
            halves.append(ref.at[b * HALF : (b + 1) * HALF, :])
    return halves


def near_kernel(slabs, near, far, notes, *refs, chunk, count):
    sources, (q_out, acc_out, peak_out) = refs[:count], refs[count : count + 3]
    refs = refs[count + 3 :]
    near_in, far_in, own, *loads = refs[: 3 + count]
    q_all, acc_all, peak_all, keys, values, scores, peak_ref, acc, sems = refs[3 + count :]
    pairs = [(sources[0].at[: 2 * HALF, :], loads[0])] + list(zip(sources[1:], loads[1:]))
    pairs += [(notes.at[0], own), (near, near_in), (far, far_in)]
    copies = fetch(pairs, sems.at[: count + 3])
    mine = slabs[lax.axis_index("key")]
    core = lax.axis_index("hid_1")
    x = lax.axis_index("hid_0")
    for copy in copies[:count]:
        copy.wait()
    chunks = gather_visible(mine, None, halves_of(loads), None, keys, values, chunk)
    for copy in copies[count:]:
        copy.wait()
    for j in range(4):
        half = x if j < 2 else 1 - x
        parity = core if j % 2 == 0 else 1 - core
        cols = pl.ds(pl.multiple_of(parity * PAIR, PAIR), PAIR)
        rows = [slice((2 * j + t) * ROWS, (2 * j + t + 1) * ROWS) for t in range(2)]

        @pl.when(half == core)
        def _(cols=cols, rows=rows):
            both = near_in[:, cols]
            q_all[rows[0], :] = both[:, :HD]
            q_all[rows[1], :] = both[:, HD:]

        @pl.when(half != core)
        def _(cols=cols, rows=rows):
            both = far_in[:, cols]
            q_all[rows[0], :] = both[:, :HD]
            q_all[rows[1], :] = both[:, HD:]

    out = fetch([(q_all, q_out)], sems.at[count + 3 : count + 4])
    zeros = jnp.zeros((NEW, HD), BF16)
    own_keys = jnp.concatenate([own[:, :HD], zeros], axis=0)
    own_values = jnp.concatenate([own[:, HD:], zeros], axis=0)
    own_values = jnp.concatenate([own_values, jnp.ones((HD, HD), BF16)], axis=1)
    row = lax.broadcasted_iota(jnp.int32, (TALL, HD), 0) % ROWS
    lane = lax.broadcasted_iota(jnp.int32, (TALL, HD), 1)
    visible = jnp.logical_and(lane < NEW, lane + new_offset() <= row)
    for step in range(8 * ROWS // TALL):
        at = pl.ds(step * TALL, TALL)
        q = q_all[at, :]
        s = lax.dot_general(q, own_keys, CONTRACT, preferred_element_type=F32)
        s = jnp.where(visible, s, NEGATIVE)
        peak_ref[...] = s

        def before(peak, s=s):
            p = jnp.where(visible, jnp.exp2((s - peak) * EXPONENT), 0.0)
            return jnp.dot(p.astype(BF16), own_values, preferred_element_type=F32)

        peak = attend(
            q, peak_ref, chunks, keys, values, scores, chunk, acc, before
        )
        acc_all[at, :] = acc[:, :HD]
        peak_all[at, :] = jnp.where(lane < HD // 2, peak, acc[:, HD:])
        first_sem = count + 4 + 2 * step
        out += fetch(
            [
                (acc_all.at[at, :], acc_out.at[at, :]),
                (peak_all.at[at, :], peak_out.at[at, :]),
            ],
            sems.at[first_sem : first_sem + 2],
        )
    for copy in out:
        copy.wait()


def attend_near(slabs, near, far, notes, loads):
    count, chunk = len(loads), 1280
    shapes = [(2 * HALF, PAIR)] + [a.shape for a in loads[1:]]
    height = sum(shape[0] // HALF * ROWS for shape in shapes)
    state = [((8 * ROWS, HD), BF16), ((8 * ROWS, HD), F32), ((8 * ROWS, HD), F32)]
    return pl.pallas_call(
        functools.partial(near_kernel, chunk=chunk, count=count),
        out_shape=[shaped(*s) for s in state],
        in_specs=[SMEM] + [HBM] * (3 + count),
        out_specs=[HBM] * 3,
        scratch_shapes=[
            pltpu.VMEM((ROWS, 4 * HD), BF16),
            pltpu.VMEM((ROWS, 4 * HD), BF16),
            pltpu.VMEM((NEW, PAIR), BF16),
            *[pltpu.VMEM(shape, BF16) for shape in shapes],
            *[pltpu.VMEM(*s) for s in state],
            pltpu.VMEM((height, HD), BF16),
            pltpu.VMEM((height, PAIR), BF16),
            pltpu.VMEM((height // chunk, TALL, chunk), F32),
            pltpu.VMEM((TALL, HD), F32),
            pltpu.VMEM((TALL, PAIR), F32),
            pltpu.SemaphoreType.DMA((count + 4 + 2 * (8 * ROWS // TALL),)),
        ],
        compiler_params=params(),
        cost_estimate=SMALL,
        name="near",
    )(slabs, near, far, notes, *loads)


def far_kernel(slabs, *refs, chunk, count):
    sources, outs = refs[: 4 + count], refs[4 + count : 7 + count]
    refs = refs[7 + count :]
    core = lax.axis_index("hid_1")
    outs = [outs[0].at[core], outs[0].at[1 - core], outs[1], outs[2]]
    buffers = refs[: 4 + count]
    queries, acc_in, peak_in, new, *loads = buffers
    keys, values, scores, peak_ref, acc, sems = refs[4 + count :]
    tall = 8 * ROWS
    copies = fetch(list(zip(sources, buffers))[::-1], sems)
    mine = slabs[lax.axis_index("key")]
    for copy in copies[: count + 1]:
        copy.wait()
    chunks = gather_visible(mine, slabs, halves_of(loads), new, keys, values, chunk)
    for copy in copies[count + 1 :]:
        copy.wait()
    peak_ref[...] = jnp.broadcast_to(peak_in[:, :1], (tall, HD))

    def before(peak):
        factor = jnp.exp2((peak_in[:, :1] - peak) * EXPONENT)
        total = jnp.broadcast_to(peak_in[:, HD // 2 : HD // 2 + 1], (tall, HD))
        return jnp.concatenate([acc_in[...], total], axis=1) * factor

    peak = attend(
        queries[...], peak_ref, chunks, keys, values, scores, chunk, acc, before
    )
    total = acc[:, HD:]
    heads = (acc[:, :HD] / jnp.where(total > 0.0, total, 1.0)).astype(BF16)
    lane = lax.broadcasted_iota(jnp.int32, (ROWS, HD), 1)
    totals = jnp.zeros((ROWS, HD), F32)
    peaks = jnp.zeros((ROWS, HD), F32)
    for h in range(tall // ROWS):
        rows = slice(h * ROWS, (h + 1) * ROWS)
        totals = jnp.where(lane == h, total[rows], totals)
        peaks = jnp.where(lane == h, peak[rows], peaks)
    some = totals > 0.0
    level = peaks * EXPONENT + jnp.log2(jnp.where(some, totals, 1.0))
    level = jnp.transpose(jnp.where(some, level, NEGATIVE))
    where = lax.broadcasted_iota(jnp.int32, (16, ROWS), 0)
    for t in range(tall // (2 * ROWS)):
        out = outs[t]
        table = jnp.zeros((16, ROWS), F32)
        for half in range(2):
            h = 2 * t + half
            cols = slice(half * HD, (half + 1) * HD)
            out[:ROWS, cols] = heads[h * ROWS : (h + 1) * ROWS]
            rest = level[h : h + 1, :]
            for k in range(3):
                coded = rest.astype(BF16).astype(F32)
                table = jnp.where(where == 3 * half + k, coded, table)
                rest = rest - coded
        out[ROWS:, :] = table.astype(BF16)


def attend_far(slabs, queries, acc, peak, new, loads):
    operands = [queries, acc, peak, new, *loads]
    count, chunk = len(loads), 1024
    height = sum(a.shape[0] // HALF * ROWS for a in loads) + 8 * NEW
    height = -(-height // chunk) * chunk
    tall = 8 * ROWS
    return pl.pallas_call(
        functools.partial(far_kernel, chunk=chunk, count=count),
        out_shape=[shaped((2, MSG, PAIR), BF16)] + [shaped((MSG, PAIR), BF16)] * 2,
        in_specs=[SMEM] + [HBM] * len(operands),
        out_specs=[VMEM] * 3,
        scratch_shapes=[
            *[pltpu.VMEM(a.shape, a.dtype) for a in operands],
            pltpu.VMEM((height, HD), BF16),
            pltpu.VMEM((height, PAIR), BF16),
            pltpu.VMEM((height // chunk, tall, chunk), F32),
            pltpu.VMEM((tall, HD), F32),
            pltpu.VMEM((tall, PAIR), F32),
            pltpu.SemaphoreType.DMA((len(operands),)),
        ],
        compiler_params=params(),
        cost_estimate=MEDIUM,
        name="far",
    )(slabs, *operands)


def merge_kernel(pair, straight, across, out):
    parts = [pair.at[0], pair.at[1], straight, across]
    levels = []
    for ref in parts:
        t = ref[ROWS:, :].astype(F32)
        levels.append([t[0:1] + t[1:2] + t[2:3], t[3:4] + t[4:5] + t[5:6]])
    rows = []
    for half in range(2):
        top = functools.reduce(jnp.maximum, [lv[half] for lv in levels])
        w = [jnp.exp2(lv[half] - top) for lv in levels]
        total = w[0] + w[1] + w[2] + w[3]
        rows.extend([x / total for x in w])
    table = jnp.concatenate(rows, axis=0)
    table = jnp.transpose(jnp.concatenate([table, jnp.zeros((HD - 8, ROWS), F32)], axis=0))
    for half in range(2):
        cols = slice(half * HD, (half + 1) * HD)
        so_far = None
        for t, ref in enumerate(parts):
            w = table[:, half * 4 + t : half * 4 + t + 1]
            term = ref[:ROWS, cols].astype(F32) * w
            so_far = term if so_far is None else so_far + term
        out[:, cols] = so_far.astype(BF16)


def merge(parts):
    return pl.pallas_call(
        merge_kernel,
        out_shape=shaped((ROWS, PAIR), BF16),
        in_specs=[VMEM] * 3,
        out_specs=VMEM,
        compiler_params=params(8),
        cost_estimate=SMALL,
        name="merge",
    )(*parts)


def project_kernel(*refs):
    heads, weights, send, keep = refs[:4], refs[4:8], refs[8], refs[9]
    core = lax.axis_index("hid_1")
    h = jnp.concatenate([ref[...] for ref in heads], axis=1)
    for out, side in ((send, 1 - core), (keep, core)):
        for t in range(4):
            cols = pl.ds(pl.multiple_of(t * 512 + side * ROWS, ROWS), ROWS)
            w = jnp.concatenate([ref[:, cols] for ref in weights], axis=0)
            total = jnp.dot(h, w, preferred_element_type=F32)
            out[:, t * ROWS : (t + 1) * ROWS] = total.astype(out.dtype)


def project(heads, weights):
    width = weights[0].shape[1]
    return pl.pallas_call(
        project_kernel,
        out_shape=[shaped((ROWS, width // 2), BF16), shaped((ROWS, width // 2), F32)],
        in_specs=[VMEM] * 8,
        out_specs=[VMEM] * 2,
        compiler_params=params(16),
        cost_estimate=SMALL,
        name="project",
    )(*heads, *weights)


def split_kernel(keep, got, own, *sends):
    spot = 2 * lax.axis_index("head_0") + lax.axis_index("hid_0")
    for by in range(4):
        cols = pl.ds(pl.multiple_of(lax.rem(spot + by, 4) * ROWS, ROWS), ROWS)
        total = keep[:, cols] + got[:, cols].astype(F32)
        if by == 0:
            own[...] = total
        else:
            sends[by - 1][...] = total.astype(BF16)


def split(keep, got):
    return pl.pallas_call(
        split_kernel,
        out_shape=[shaped((ROWS, ROWS), F32)] + [shaped((ROWS, ROWS), BF16)] * 3,
        in_specs=[VMEM] * 2,
        out_specs=[VMEM] * 4,
        compiler_params=params(8),
        cost_estimate=SMALL,
        name="split",
    )(keep, got)


def body(
    tokens,
    query_weight,
    key_weight,
    value_weight,
    output_weight,
    key_cache,
    value_cache,
    cache_places,
    slab_places,
):

    load, spots = pack(
        cache_places, slab_places, key_cache.reshape(-1, HD), value_cache.reshape(-1, HD)
    )

    def away(array, by):
        pairs = []
        for k in range(8):
            pairs.append((2 * k, 2 * ((k + by) % 8)))
            pairs.append((2 * k + 1, 2 * ((k - by) % 8) + 1))
        return lax.ppermute(array, ("key", "hid_1"), pairs)

    one = away(load, 1)

    pieces = columns(output_weight)

    send, keep = first(tokens, query_weight, key_weight, value_weight)
    one, keep, pieces = lax.optimization_barrier((one, keep, pieces))
    two = away(one, 1)
    send, keep = second(keep, swap(send, "hid_1"))
    got = swap(send, "hid_0")
    weights = [pieces[3]]
    for piece, by in zip(pieces, (2, 1, 3)):
        weights.append(lax.ppermute(piece, "head_1", shift(4, by)))

    middle = HD // 2
    index = np.arange(HD) % middle
    frequency = jnp.exp(jnp.asarray(index, F32) * (-2.0 * math.log(THETA) / HD))
    sign = np.where(np.arange(HD) < middle, -1.0, 1.0).astype(np.float32)
    angles = spots * frequency[None, :]
    cosine, sine = jnp.cos(angles), jnp.sin(angles) * sign[None, :]
    two, cosine, sine = lax.optimization_barrier((two, cosine, sine))
    three = away(two, 1)
    queries, notes = rotated(keep, got, cosine, sine)
    far = swap(queries, "hid_1")
    far, onward = lax.optimization_barrier((far, two[: 2 * HALF]))
    four = away(onward, 2)

    new = lax.all_to_all(notes, "key", split_axis=0, concat_axis=0, tiled=True)

    state = attend_near(slab_places, queries, far, notes, [load, one, two])
    pair, straight, across = attend_far(slab_places, *state, new, [three, four])
    parts = [
        lax.all_to_all(pair, "hid_1", split_axis=0, concat_axis=0, tiled=True),
        swap(straight, "hid_0"),
        lax.ppermute(across, HID, [(0, 3), (1, 2), (2, 1), (3, 0)]),
    ]
    parts, weights = lax.optimization_barrier((parts, weights))
    merged = merge(parts)

    heads = [merged] + [lax.ppermute(merged, "head_1", shift(4, by)) for by in (2, 1, 3)]
    send, keep = project(heads, weights)
    own, *blocks = split(keep, swap(send, "hid_1"))
    out = own
    for by in (2, 1, 3):
        out = out + lax.ppermute(blocks[by - 1], ALONG_X, shift(4, by)).astype(F32)
    return out.astype(BF16)


def solution(mesh):
    finer = Mesh(
        mesh.devices.reshape(2, 4, mesh.shape["key"], 2, 2),
        ("head_0", "head_1", "key", "hid_0", "hid_1"),
    )
    return jax.shard_map(
        body,
        mesh=finer,
        in_specs=(
            P("key", HID),
            P(HID, HEAD),
            P(HID, HEAD),
            P(HID, HEAD),
            P(HEAD_HID, None),
            P("key", HEAD, None),
            P("key", HEAD, None),
            P("key"),
            P(),
        ),
        out_specs=P("key", HEAD_HID),
        check_vma=False,
    )
```

profile of v0, /device:TPU:1, one launch (start us, length us, event | category | flops | bytes accessed | tf_op | source)
XLA Modules:
  0.0 100.8 jit_solution(3420788895932994430)
XLA Ops:
  0.0 3.2 %pack.1 = (bf16[1088,256]{1,0:T(8,128)(2,1)}, f32[256,128]{1,0:T(8,128)}) custom-call(s32[8]{0:T(128)} %places.1, s32[8]{0:T(128)} %slabs.5, bf16[2048,128]{1,0:T(8,128)(2,1)} %bitcast.2, bf16[2048,128]{1,0:T(8,128)(2,1)} %bitcast.3), custom_call_target="tpu_custom_call" | custom-call | flops 1 | bytes 1 | tf_op jit(solution)/shard_map/pack/pallas_call | solution.py:101
  3.2 0.0 copy-start.3
  3.2 0.0 copy-start.4
  3.2 0.0 copy-start.5
  3.3 6.5 %collective-permute-start = (bf16[1088,256]{1,0:T(8,128)(2,1)}, bf16[1088,256]{1,0:T(8,128)(2,1)}, u32[]{:S(2)}, u32[]{:S(2)}) collective-permute-start(bf16[1088,256]{1,0:T(8,128)(2,1)} %get-tuple-element.47.refs_0_), channel_id=1, source_target_pairs={{0,4},{1,29},{4,8},{5,1},{8,12},{9,5},{12,16},{13,9},{16,20},{17,1... | collective-permute-start | bytes 1671176 | tf_op jit(solution)/shard_map/ppermute | solution.py:634
  9.7 4.6 %first.1 = (bf16[320,512]{1,0:T(8,128)(2,1)}, f32[320,512]{1,0:T(8,128)}) custom-call(bf16[256,2048]{1,0:T(8,128)(2,1)} %tokens.1, bf16[2048,1024]{1,0:T(8,128)(2,1)} %query.1, bf16[2048,128]{1,0:T(8,128)(2,1)} %key.1, bf16[2048,128]{1,0:T(8,128)(2,1)} %value.1), custom_call_target="tpu_custom_call" | custom-call | flops 1 | bytes 1 | tf_op jit(solution)/shard_map/first/pallas_call | solution.py:192
  14.3 0.1 collective-permute-start.1
  14.4 3.5 %columns.1 = (bf16[256,2048]{1,0:T(8,128)(2,1)}, bf16[256,2048]{1,0:T(8,128)(2,1)}, bf16[256,2048]{1,0:T(8,128)(2,1)}, bf16[256,2048]{1,0:T(8,128)(2,1)}) custom-call(bf16[256,8192]{1,0:T(8,128)(2,1)} %weight.1), custom_call_target="tpu_custom_call" | custom-call | flops 1 | bytes 1 | tf_op jit(solution)/shard_map/columns/pallas_call | solution.py:133
  17.9 1.8 %collective-permute-start.3 = (bf16[1088,256]{1,0:T(8,128)(2,1)}, bf16[1088,256]{1,0:T(8,128)(2,1)}, u32[]{:S(2)}, u32[]{:S(2)}) collective-permute-start(bf16[1088,256]{1,0:T(8,128)(2,1)} %collective-permute-done.refs_1_), channel_id=1, source_target_pairs={{0,4},{1,29},{4,8},{5,1},{8,12},{9,5},{12,16},{13,9},{16,20},{17,1... | collective-permute-start | bytes 1671176 | tf_op jit(solution)/shard_map/ppermute | solution.py:634
  19.7 1.3 %collective-permute-start.10 = (bf16[256,2048]{1,0:T(8,128)(2,1)}, bf16[256,2048]{1,0:T(8,128)(2,1)S(1)}, u32[]{:S(2)}, u32[]{:S(2)}) collective-permute-start(bf16[256,2048]{1,0:T(8,128)(2,1)} %get-tuple-element.74), channel_id=1, source_target_pairs={{0,32},{32,64},{64,96},{96,0},{1,33},{33,65},{65,97},{97,1},{2,34}... | collective-permute-start | bytes 3145736 | tf_op jit(solution)/shard_map/ppermute | solution.py:647
  20.9 1.4 %collective-permute-start.11 = (bf16[256,2048]{1,0:T(8,128)(2,1)}, bf16[256,2048]{1,0:T(8,128)(2,1)S(1)}, u32[]{:S(2)}, u32[]{:S(2)}) collective-permute-start(bf16[256,2048]{1,0:T(8,128)(2,1)} %get-tuple-element.75), channel_id=1, source_target_pairs={{0,96},{32,0},{64,32},{96,64},{1,97},{33,1},{65,33},{97,65},{2,98}... | collective-permute-start | bytes 3145736 | tf_op jit(solution)/shard_map/ppermute | solution.py:647
  22.4 1.6 %collective-permute-start.9 = (bf16[256,2048]{1,0:T(8,128)(2,1)}, bf16[256,2048]{1,0:T(8,128)(2,1)}, u32[]{:S(2)}, u32[]{:S(2)}) collective-permute-start(bf16[256,2048]{1,0:T(8,128)(2,1)} %get-tuple-element.73), channel_id=1, source_target_pairs={{0,64},{32,96},{64,0},{96,32},{1,65},{33,97},{65,1},{97,33},{2,66}... | collective-permute-start | bytes 3145736 | tf_op jit(solution)/shard_map/ppermute | solution.py:647
  24.0 0.1 second.1
  24.1 1.3 %collective-permute-start.2 = (bf16[288,512]{1,0:T(8,128)(2,1)S(1)}, bf16[288,512]{1,0:T(8,128)(2,1)S(1)}, u32[]{:S(2)}, u32[]{:S(2)}) collective-permute-start(bf16[288,512]{1,0:T(8,128)(2,1)S(1)} %get-tuple-element.56), channel_id=1, source_target_pairs={{0,2},{2,0},{1,3},{3,1},{4,6},{6,4},{5,7},{7,5},{8,10},{10,8},{9,1... | collective-permute-start | bytes 884744 | tf_op jit(solution)/shard_map/ppermute | solution.py:57
  25.4 0.5 sine_multiply_fusion
  25.9 1.1 %collective-permute-done.3.refs_2_ = bf16[1088,256]{1,0:T(8,128)(2,1)} collective-permute-done((bf16[1088,256]{1,0:T(8,128)(2,1)}, bf16[1088,256]{1,0:T(8,128)(2,1)}, u32[]{:S(2)}, u32[]{:S(2)}) %collective-permute-start.3) | collective-permute-done | bytes 557088 | tf_op jit(solution)/shard_map/ppermute | solution.py:634
  27.0 2.8 %collective-permute-start.5 = (bf16[1088,256]{1,0:T(8,128)(2,1)}, bf16[1088,256]{1,0:T(8,128)(2,1)}, u32[]{:S(2)}, u32[]{:S(2)}) collective-permute-start(bf16[1088,256]{1,0:T(8,128)(2,1)} %collective-permute-done.3.refs_2_), channel_id=1, source_target_pairs={{0,4},{1,29},{4,8},{5,1},{8,12},{9,5},{12,16},{13,9},{16,20},{17,1... | collective-permute-start | bytes 1671176 | tf_op jit(solution)/shard_map/ppermute | solution.py:634
  29.8 3.3 %collective-permute-done.2.got = bf16[288,512]{1,0:T(8,128)(2,1)S(1)} collective-permute-done((bf16[288,512]{1,0:T(8,128)(2,1)S(1)}, bf16[288,512]{1,0:T(8,128)(2,1)S(1)}, u32[]{:S(2)}, u32[]{:S(2)}) %collective-permute-start.2) | collective-permute-done | bytes 294944 | tf_op jit(solution)/shard_map/ppermute | solution.py:57
  33.0 1.0 %rotated.1 = (bf16[256,512]{1,0:T(8,128)(2,1)}, bf16[8,64,256]{2,1,0:T(8,128)(2,1)}) custom-call(f32[288,512]{1,0:T(8,128)S(1)} %get-tuple-element.55.keep, bf16[288,512]{1,0:T(8,128)(2,1)S(1)} %collective-permute-done.2.got, f32[256,128]{1,0:T(8,128)S(1)} %get-tuple-element.59.cosine, f32[256,128]{1,0:T(8,128)S(1)} %get-tuple-element.60.sine), custom_call_target="tpu_custom_call" | custom-call | flops 1 | bytes 1 | tf_op jit(solution)/shard_map/rotated/pallas_call | solution.py:258
  34.1 0.6 collective-permute-start.4
  34.7 4.6 %all-to-all-start = ((bf16[8,64,256]{2,1,0:T(8,128)(2,1)}), bf16[8,64,256]{2,1,0:T(8,128)(2,1)S(1)}, u32[]{:S(2)}, u32[]{:S(2)}) async-start(bf16[8,64,256]{2,1,0:T(8,128)(2,1)} %get-tuple-element.64.notes), calls=%async_computation | async-start | bytes 524288 | tf_op jit(solution)/shard_map/all_to_all | solution.py:662
  39.2 1.7 %slice.3 = bf16[544,256]{1,0:T(8,128)(2,1)} slice(bf16[1088,256]{1,0:T(8,128)(2,1)} %collective-permute-done.3.refs_2_), slice={[0:544], [0:256]} | slice | bytes 557056 | tf_op jit(solution)/shard_map/slice | solution.py:659
  40.9 0.0 collective-permute-done.4.far
  40.9 3.6 %collective-permute-start.6 = (bf16[544,256]{1,0:T(8,128)(2,1)}, bf16[544,256]{1,0:T(8,128)(2,1)}, u32[]{:S(2)}, u32[]{:S(2)}) collective-permute-start(bf16[544,256]{1,0:T(8,128)(2,1)} %slice.3), channel_id=1, source_target_pairs={{0,8},{1,25},{4,12},{5,29},{8,16},{9,1},{12,20},{13,5},{16,24},{17... | collective-permute-start | bytes 835592 | tf_op jit(solution)/shard_map/ppermute | solution.py:634
  44.5 8.4 %near.1 = (bf16[2048,128]{1,0:T(8,128)(2,1)}, f32[2048,128]{1,0:T(8,128)}, f32[2048,128]{1,0:T(8,128)}) custom-call(s32[8]{0:T(128)} %slabs.5, bf16[256,512]{1,0:T(8,128)(2,1)} %get-tuple-element.61.near, bf16[256,512]{1,0:T(8,128)(2,1)} %collective-permute-done.4.far, bf16[8,64,256]{2,1,0:T(8,128)(2,1)} %get-tuple-element.64.notes, ...), custom_call_target="tpu_custom_call" | custom-call | flops 1 | bytes 1 | tf_op jit(solution)/shard_map/near/pallas_call | solution.py:425
  53.0 1.8 %collective-permute-done.6.refs_5_ = bf16[544,256]{1,0:T(8,128)(2,1)} collective-permute-done((bf16[544,256]{1,0:T(8,128)(2,1)}, bf16[544,256]{1,0:T(8,128)(2,1)}, u32[]{:S(2)}, u32[]{:S(2)}) %collective-permute-start.6) | collective-permute-done | bytes 278560 | tf_op jit(solution)/shard_map/ppermute | solution.py:634
  54.7 10.4 %far.1 = (bf16[2,272,256]{2,1,0:T(8,128)(2,1)}, bf16[272,256]{1,0:T(8,128)(2,1)}, bf16[272,256]{1,0:T(8,128)(2,1)}) custom-call(s32[8]{0:T(128)} %slabs.5, bf16[2048,128]{1,0:T(8,128)(2,1)} %get-tuple-element.65.refs_0_, f32[2048,128]{1,0:T(8,128)} %get-tuple-element.66.refs_1_, f32[2048,128]{1,0:T(8,128)} %get-tuple-element.67.refs_2_, ...), custom_call_target="tpu_custom_call" | custom-call | flops 134217728 | bytes 262144 | tf_op jit(solution)/shard_map/far/pallas_call | solution.py:509
  65.2 1.0 collective-permute-start.7
  66.2 2.7 %collective-permute-start.8 = (bf16[272,256]{1,0:T(8,128)(2,1)}, bf16[272,256]{1,0:T(8,128)(2,1)}, u32[]{:S(2)}, u32[]{:S(2)}) collective-permute-start(bf16[272,256]{1,0:T(8,128)(2,1)} %get-tuple-element.71), channel_id=1, source_target_pairs={{0,3},{1,2},{2,1},{3,0},{4,7},{5,6},{6,5},{7,4},{8,11},{9,10},{10,... | collective-permute-start | bytes 417800 | tf_op jit(solution)/shard_map/ppermute | solution.py:669
  68.9 3.4 %all-to-all-start.1 = ((bf16[2,272,256]{2,1,0:T(8,128)(2,1)}), bf16[2,272,256]{2,1,0:T(8,128)(2,1)S(1)}, u32[]{:S(2)}, u32[]{:S(2)}) async-start(bf16[2,272,256]{2,1,0:T(8,128)(2,1)} %get-tuple-element.69), calls=%async_computation.1 | async-start | bytes 557056 | tf_op jit(solution)/shard_map/all_to_all | solution.py:667
  72.4 0.0 collective-permute-done.11.refs_7_
  72.4 1.2 %all-to-all-done.1.pair = bf16[2,272,256]{2,1,0:T(8,128)(2,1)S(1)} async-done(((bf16[2,272,256]{2,1,0:T(8,128)(2,1)}), bf16[2,272,256]{2,1,0:T(8,128)(2,1)S(1)}, u32[]{:S(2)}, u32[]{:S(2)}) %all-to-all-start.1) | async-done | bytes 278560 | tf_op jit(solution)/shard_map/all_to_all | solution.py:667
  73.6 0.9 collective-permute-done.8.across
  74.5 1.5 %merge.1.refs_0_ = bf16[256,256]{1,0:T(8,128)(2,1)S(1)} custom-call(bf16[2,272,256]{2,1,0:T(8,128)(2,1)S(1)} %all-to-all-done.1.pair, bf16[272,256]{1,0:T(8,128)(2,1)} %collective-permute-done.7.straight, bf16[272,256]{1,0:T(8,128)(2,1)} %collective-permute-done.8.across), custom_call_target="tpu_custom_call" | custom-call | flops 1 | bytes 1 | tf_op jit(solution)/shard_map/merge/pallas_call | solution.py:554
  76.0 1.4 %collective-permute-start.12 = (bf16[256,256]{1,0:T(8,128)(2,1)S(1)}, bf16[256,256]{1,0:T(8,128)(2,1)S(1)}, u32[]{:S(2)}, u32[]{:S(2)}) collective-permute-start(bf16[256,256]{1,0:T(8,128)(2,1)S(1)} %merge.1.refs_0_), channel_id=1, source_target_pairs={{0,64},{32,96},{64,0},{96,32},{1,65},{33,97},{65,1},{97,33},{2,66}... | collective-permute-start | bytes 393224 | tf_op jit(solution)/shard_map/ppermute | solution.py:674
  77.4 0.1 collective-permute-start.13
  77.5 2.6 %collective-permute-start.14 = (bf16[256,256]{1,0:T(8,128)(2,1)S(1)}, bf16[256,256]{1,0:T(8,128)(2,1)S(1)}, u32[]{:S(2)}, u32[]{:S(2)}) collective-permute-start(bf16[256,256]{1,0:T(8,128)(2,1)S(1)} %merge.1.refs_0_), channel_id=1, source_target_pairs={{0,96},{32,0},{64,32},{96,64},{1,97},{33,1},{65,33},{97,65},{2,98}... | collective-permute-start | bytes 393224 | tf_op jit(solution)/shard_map/ppermute | solution.py:674
  80.1 2.9 %collective-permute-done.12.refs_1_ = bf16[256,256]{1,0:T(8,128)(2,1)S(1)} collective-permute-done((bf16[256,256]{1,0:T(8,128)(2,1)S(1)}, bf16[256,256]{1,0:T(8,128)(2,1)S(1)}, u32[]{:S(2)}, u32[]{:S(2)}) %collective-permute-start.12) | collective-permute-done | bytes 131104 | tf_op jit(solution)/shard_map/ppermute | solution.py:674
  83.0 2.9 %collective-permute-done.13.refs_2_ = bf16[256,256]{1,0:T(8,128)(2,1)S(1)} collective-permute-done((bf16[256,256]{1,0:T(8,128)(2,1)S(1)}, bf16[256,256]{1,0:T(8,128)(2,1)S(1)}, u32[]{:S(2)}, u32[]{:S(2)}) %collective-permute-start.13) | collective-permute-done | bytes 131104 | tf_op jit(solution)/shard_map/ppermute | solution.py:674
  85.8 2.5 %project.1 = (bf16[256,1024]{1,0:T(8,128)(2,1)S(1)}, f32[256,1024]{1,0:T(8,128)S(1)}) custom-call(bf16[256,256]{1,0:T(8,128)(2,1)S(1)} %merge.1.refs_0_, bf16[256,256]{1,0:T(8,128)(2,1)S(1)} %collective-permute-done.12.refs_1_, bf16[256,256]{1,0:T(8,128)(2,1)S(1)} %collective-permute-done.13.refs_2_, bf16[256,256]{1,0:T(8,128)(2,1)S(1)} %collective-permute-done.14.refs_3_, ...), custom_call_target="tpu_custom_call" | custom-call | flops 1 | bytes 1 | tf_op jit(solution)/shard_map/project/pallas_call | solution.py:579
  88.4 0.5 collective-permute-start.15
  88.9 1.5 %collective-permute-done.15.got = bf16[256,1024]{1,0:T(8,128)(2,1)S(1)} collective-permute-done((bf16[256,1024]{1,0:T(8,128)(2,1)S(1)}, bf16[256,1024]{1,0:T(8,128)(2,1)S(1)}, u32[]{:S(2)}, u32[]{:S(2)}) %collective-permute-start.15) | collective-permute-done | bytes 524320 | tf_op jit(solution)/shard_map/ppermute | solution.py:57
  90.4 0.1 split.1
  90.5 2.8 %collective-permute-start.16 = (bf16[256,256]{1,0:T(8,128)(2,1)S(1)}, bf16[256,256]{1,0:T(8,128)(2,1)S(1)}, u32[]{:S(2)}, u32[]{:S(2)}) collective-permute-start(bf16[256,256]{1,0:T(8,128)(2,1)S(1)} %get-tuple-element.86), channel_id=1, source_target_pairs={{0,128},{2,130},{128,0},{130,2},{1,129},{3,131},{129,1},{131,3},{4... | collective-permute-start | bytes 393224 | tf_op jit(solution)/shard_map/ppermute | solution.py:679
  93.4 2.7 %collective-permute-start.18 = (bf16[256,256]{1,0:T(8,128)(2,1)S(1)}, bf16[256,256]{1,0:T(8,128)(2,1)S(1)}, u32[]{:S(2)}, u32[]{:S(2)}) collective-permute-start(bf16[256,256]{1,0:T(8,128)(2,1)S(1)} %get-tuple-element.88), channel_id=1, source_target_pairs={{0,130},{2,0},{128,2},{130,128},{1,131},{3,1},{129,3},{131,129},{4... | collective-permute-start | bytes 393224 | tf_op jit(solution)/shard_map/ppermute | solution.py:679
  96.1 0.8 collective-permute-done.16
  96.9 3.3 %collective-permute-done.17 = bf16[256,256]{1,0:T(8,128)(2,1)S(1)} collective-permute-done((bf16[256,256]{1,0:T(8,128)(2,1)S(1)}, bf16[256,256]{1,0:T(8,128)(2,1)S(1)}, u32[]{:S(2)}, u32[]{:S(2)}) %collective-permute-start.17) | collective-permute-done | bytes 131104 | tf_op jit(solution)/shard_map/ppermute | solution.py:679
  100.1 0.7 add_convert_fusion
  (19 shorter events, 0.0 us)
Async XLA Ops:
  3.2 22.2 %copy-start.3 = (f32[256,128]{1,0:T(8,128)S(1)}, f32[256,128]{1,0:T(8,128)}, u32[]{:S(2)}) copy-start(f32[256,128]{1,0:T(8,128)} %get-tuple-element.58) | copy-start | bytes 393220
  3.2 22.2 %copy-start.4 = (f32[128]{0:T(128)S(1)}, f32[128]{0:T(128)}, u32[]{:S(2)}) copy-start(f32[128]{0:T(128)} %constant.11) | copy-start | bytes 1540
  3.2 22.2 %copy-start.5 = (f32[128]{0:T(128)S(1)}, f32[128]{0:T(128)}, u32[]{:S(2)}) copy-start(f32[128]{0:T(128)} %constant.12) | copy-start | bytes 1540
  3.3 14.6 %collective-permute-start = (bf16[1088,256]{1,0:T(8,128)(2,1)}, bf16[1088,256]{1,0:T(8,128)(2,1)}, u32[]{:S(2)}, u32[]{:S(2)}) collective-permute-start(bf16[1088,256]{1,0:T(8,128)(2,1)} %get-tuple-element.47.refs_0_), channel_id=1, source_target_pairs={{0,4},{1,29},{4,8},{5,1},{8,12},{9,5},{12,16},{13,9},{16,20},{17,1... | collective-permute-start | bytes 1671176 | tf_op jit(solution)/shard_map/ppermute | solution.py:634
  14.3 9.7 %copy-start.1 = (f32[320,512]{1,0:T(8,128)S(1)}, f32[320,512]{1,0:T(8,128)}, u32[]{:S(2)}) copy-start(f32[320,512]{1,0:T(8,128)} %get-tuple-element.53.keep) | copy-start | bytes 1966084
  14.3 9.7 %collective-permute-start.1 = (bf16[320,512]{1,0:T(8,128)(2,1)}, bf16[320,512]{1,0:T(8,128)(2,1)S(1)}, u32[]{:S(2)}, u32[]{:S(2)}) collective-permute-start(bf16[320,512]{1,0:T(8,128)(2,1)} %get-tuple-element.54), channel_id=1, source_target_pairs={{0,1},{1,0},{2,3},{3,2},{4,5},{5,4},{6,7},{7,6},{8,9},{9,8},{10,11... | collective-permute-start | bytes 983048 | tf_op jit(solution)/shard_map/ppermute | solution.py:57
  17.9 9.1 %collective-permute-start.3 = (bf16[1088,256]{1,0:T(8,128)(2,1)}, bf16[1088,256]{1,0:T(8,128)(2,1)}, u32[]{:S(2)}, u32[]{:S(2)}) collective-permute-start(bf16[1088,256]{1,0:T(8,128)(2,1)} %collective-permute-done.refs_1_), channel_id=1, source_target_pairs={{0,4},{1,29},{4,8},{5,1},{8,12},{9,5},{12,16},{13,9},{16,20},{17,1... | collective-permute-start | bytes 1671176 | tf_op jit(solution)/shard_map/ppermute | solution.py:634
  19.7 52.7 %collective-permute-start.10 = (bf16[256,2048]{1,0:T(8,128)(2,1)}, bf16[256,2048]{1,0:T(8,128)(2,1)S(1)}, u32[]{:S(2)}, u32[]{:S(2)}) collective-permute-start(bf16[256,2048]{1,0:T(8,128)(2,1)} %get-tuple-element.74), channel_id=1, source_target_pairs={{0,32},{32,64},{64,96},{96,0},{1,33},{33,65},{65,97},{97,1},{2,34}... | collective-permute-start | bytes 3145736 | tf_op jit(solution)/shard_map/ppermute | solution.py:647
  20.9 51.4 %collective-permute-start.11 = (bf16[256,2048]{1,0:T(8,128)(2,1)}, bf16[256,2048]{1,0:T(8,128)(2,1)S(1)}, u32[]{:S(2)}, u32[]{:S(2)}) collective-permute-start(bf16[256,2048]{1,0:T(8,128)(2,1)} %get-tuple-element.75), channel_id=1, source_target_pairs={{0,96},{32,0},{64,32},{96,64},{1,97},{33,1},{65,33},{97,65},{2,98}... | collective-permute-start | bytes 3145736 | tf_op jit(solution)/shard_map/ppermute | solution.py:647
  22.4 50.0 %collective-permute-start.9 = (bf16[256,2048]{1,0:T(8,128)(2,1)}, bf16[256,2048]{1,0:T(8,128)(2,1)}, u32[]{:S(2)}, u32[]{:S(2)}) collective-permute-start(bf16[256,2048]{1,0:T(8,128)(2,1)} %get-tuple-element.73), channel_id=1, source_target_pairs={{0,64},{32,96},{64,0},{96,32},{1,65},{33,97},{65,1},{97,33},{2,66}... | collective-permute-start | bytes 3145736 | tf_op jit(solution)/shard_map/ppermute | solution.py:647
  24.1 8.9 %collective-permute-start.2 = (bf16[288,512]{1,0:T(8,128)(2,1)S(1)}, bf16[288,512]{1,0:T(8,128)(2,1)S(1)}, u32[]{:S(2)}, u32[]{:S(2)}) collective-permute-start(bf16[288,512]{1,0:T(8,128)(2,1)S(1)} %get-tuple-element.56), channel_id=1, source_target_pairs={{0,2},{2,0},{1,3},{3,1},{4,6},{6,4},{5,7},{7,5},{8,10},{10,8},{9,1... | collective-permute-start | bytes 884744 | tf_op jit(solution)/shard_map/ppermute | solution.py:57
  27.0 27.8 %collective-permute-start.5 = (bf16[1088,256]{1,0:T(8,128)(2,1)}, bf16[1088,256]{1,0:T(8,128)(2,1)}, u32[]{:S(2)}, u32[]{:S(2)}) collective-permute-start(bf16[1088,256]{1,0:T(8,128)(2,1)} %collective-permute-done.3.refs_2_), channel_id=1, source_target_pairs={{0,4},{1,29},{4,8},{5,1},{8,12},{9,5},{12,16},{13,9},{16,20},{17,1... | collective-permute-start | bytes 1671176 | tf_op jit(solution)/shard_map/ppermute | solution.py:634
  34.1 6.9 %collective-permute-start.4 = (bf16[256,512]{1,0:T(8,128)(2,1)}, bf16[256,512]{1,0:T(8,128)(2,1)}, u32[]{:S(2)}, u32[]{:S(2)}) collective-permute-start(bf16[256,512]{1,0:T(8,128)(2,1)} %get-tuple-element.61.near), channel_id=1, source_target_pairs={{0,1},{1,0},{2,3},{3,2},{4,5},{5,4},{6,7},{7,6},{8,9},{9,8},{10,11... | collective-permute-start | bytes 786440 | tf_op jit(solution)/shard_map/ppermute | solution.py:57
  34.7 51.2 %copy-start = (bf16[256,2048]{1,0:T(8,128)(2,1)S(1)}, bf16[256,2048]{1,0:T(8,128)(2,1)}, u32[]{:S(2)}) copy-start(bf16[256,2048]{1,0:T(8,128)(2,1)} %get-tuple-element.79.refs_4_) | copy-start | bytes 3145732
  34.7 18.3 %all-to-all-start = ((bf16[8,64,256]{2,1,0:T(8,128)(2,1)}), bf16[8,64,256]{2,1,0:T(8,128)(2,1)S(1)}, u32[]{:S(2)}, u32[]{:S(2)}) async-start(bf16[8,64,256]{2,1,0:T(8,128)(2,1)} %get-tuple-element.64.notes), calls=%async_computation | async-start | bytes 524288 | tf_op jit(solution)/shard_map/all_to_all | solution.py:662
  40.9 13.8 %collective-permute-start.6 = (bf16[544,256]{1,0:T(8,128)(2,1)}, bf16[544,256]{1,0:T(8,128)(2,1)}, u32[]{:S(2)}, u32[]{:S(2)}) collective-permute-start(bf16[544,256]{1,0:T(8,128)(2,1)} %slice.3), channel_id=1, source_target_pairs={{0,8},{1,25},{4,12},{5,29},{8,16},{9,1},{12,20},{13,5},{16,24},{17... | collective-permute-start | bytes 835592 | tf_op jit(solution)/shard_map/ppermute | solution.py:634
  52.9 1.8 %copy-start.2 = (bf16[8,64,256]{2,1,0:T(8,128)(2,1)}, bf16[8,64,256]{2,1,0:T(8,128)(2,1)S(1)}, u32[]{:S(2)}) copy-start(bf16[8,64,256]{2,1,0:T(8,128)(2,1)S(1)} %all-to-all-done.refs_3_) | copy-start | bytes 786436
  65.2 8.4 %collective-permute-start.7 = (bf16[272,256]{1,0:T(8,128)(2,1)}, bf16[272,256]{1,0:T(8,128)(2,1)}, u32[]{:S(2)}, u32[]{:S(2)}) collective-permute-start(bf16[272,256]{1,0:T(8,128)(2,1)} %get-tuple-element.70), channel_id=1, source_target_pairs={{0,2},{2,0},{1,3},{3,1},{4,6},{6,4},{5,7},{7,5},{8,10},{10,8},{9,1... | collective-permute-start | bytes 417800 | tf_op jit(solution)/shard_map/ppermute | solution.py:57
  66.2 8.3 %collective-permute-start.8 = (bf16[272,256]{1,0:T(8,128)(2,1)}, bf16[272,256]{1,0:T(8,128)(2,1)}, u32[]{:S(2)}, u32[]{:S(2)}) collective-permute-start(bf16[272,256]{1,0:T(8,128)(2,1)} %get-tuple-element.71), channel_id=1, source_target_pairs={{0,3},{1,2},{2,1},{3,0},{4,7},{5,6},{6,5},{7,4},{8,11},{9,10},{10,... | collective-permute-start | bytes 417800 | tf_op jit(solution)/shard_map/ppermute | solution.py:669
  68.9 4.6 %all-to-all-start.1 = ((bf16[2,272,256]{2,1,0:T(8,128)(2,1)}), bf16[2,272,256]{2,1,0:T(8,128)(2,1)S(1)}, u32[]{:S(2)}, u32[]{:S(2)}) async-start(bf16[2,272,256]{2,1,0:T(8,128)(2,1)} %get-tuple-element.69), calls=%async_computation.1 | async-start | bytes 557056 | tf_op jit(solution)/shard_map/all_to_all | solution.py:667
  76.0 7.0 %collective-permute-start.12 = (bf16[256,256]{1,0:T(8,128)(2,1)S(1)}, bf16[256,256]{1,0:T(8,128)(2,1)S(1)}, u32[]{:S(2)}, u32[]{:S(2)}) collective-permute-start(bf16[256,256]{1,0:T(8,128)(2,1)S(1)} %merge.1.refs_0_), channel_id=1, source_target_pairs={{0,64},{32,96},{64,0},{96,32},{1,65},{33,97},{65,1},{97,33},{2,66}... | collective-permute-start | bytes 393224 | tf_op jit(solution)/shard_map/ppermute | solution.py:674
  77.4 8.4 %collective-permute-start.13 = (bf16[256,256]{1,0:T(8,128)(2,1)S(1)}, bf16[256,256]{1,0:T(8,128)(2,1)S(1)}, u32[]{:S(2)}, u32[]{:S(2)}) collective-permute-start(bf16[256,256]{1,0:T(8,128)(2,1)S(1)} %merge.1.refs_0_), channel_id=1, source_target_pairs={{0,32},{32,64},{64,96},{96,0},{1,33},{33,65},{65,97},{97,1},{2,34}... | collective-permute-start | bytes 393224 | tf_op jit(solution)/shard_map/ppermute | solution.py:674
  77.5 8.4 %collective-permute-start.14 = (bf16[256,256]{1,0:T(8,128)(2,1)S(1)}, bf16[256,256]{1,0:T(8,128)(2,1)S(1)}, u32[]{:S(2)}, u32[]{:S(2)}) collective-permute-start(bf16[256,256]{1,0:T(8,128)(2,1)S(1)} %merge.1.refs_0_), channel_id=1, source_target_pairs={{0,96},{32,0},{64,32},{96,64},{1,97},{33,1},{65,33},{97,65},{2,98}... | collective-permute-start | bytes 393224 | tf_op jit(solution)/shard_map/ppermute | solution.py:674
  88.4 2.0 %collective-permute-start.15 = (bf16[256,1024]{1,0:T(8,128)(2,1)S(1)}, bf16[256,1024]{1,0:T(8,128)(2,1)S(1)}, u32[]{:S(2)}, u32[]{:S(2)}) collective-permute-start(bf16[256,1024]{1,0:T(8,128)(2,1)S(1)} %get-tuple-element.84), channel_id=1, source_target_pairs={{0,1},{1,0},{2,3},{3,2},{4,5},{5,4},{6,7},{7,6},{8,9},{9,8},{10,11... | collective-permute-start | bytes 1572872 | tf_op jit(solution)/shard_map/ppermute | solution.py:57
  90.5 6.3 %collective-permute-start.16 = (bf16[256,256]{1,0:T(8,128)(2,1)S(1)}, bf16[256,256]{1,0:T(8,128)(2,1)S(1)}, u32[]{:S(2)}, u32[]{:S(2)}) collective-permute-start(bf16[256,256]{1,0:T(8,128)(2,1)S(1)} %get-tuple-element.86), channel_id=1, source_target_pairs={{0,128},{2,130},{128,0},{130,2},{1,129},{3,131},{129,1},{131,3},{4... | collective-permute-start | bytes 393224 | tf_op jit(solution)/shard_map/ppermute | solution.py:679
  93.4 6.7 %collective-permute-start.17 = (bf16[256,256]{1,0:T(8,128)(2,1)S(1)}, bf16[256,256]{1,0:T(8,128)(2,1)S(1)}, u32[]{:S(2)}, u32[]{:S(2)}) collective-permute-start(bf16[256,256]{1,0:T(8,128)(2,1)S(1)} %get-tuple-element.87), channel_id=1, source_target_pairs={{0,2},{2,128},{128,130},{130,0},{1,3},{3,129},{129,131},{131,1},{4... | collective-permute-start | bytes 393224 | tf_op jit(solution)/shard_map/ppermute | solution.py:679
  93.4 6.7 %collective-permute-start.18 = (bf16[256,256]{1,0:T(8,128)(2,1)S(1)}, bf16[256,256]{1,0:T(8,128)(2,1)S(1)}, u32[]{:S(2)}, u32[]{:S(2)}) collective-permute-start(bf16[256,256]{1,0:T(8,128)(2,1)S(1)} %get-tuple-element.88), channel_id=1, source_target_pairs={{0,130},{2,0},{128,2},{130,128},{1,131},{3,1},{129,3},{131,129},{4... | collective-permute-start | bytes 393224 | tf_op jit(solution)/shard_map/ppermute | solution.py:679
where the time goes:
time: 103 us; the launch traced here: 101 us
  starting transfers between devices  42.8 us (42%)
  Pallas kernels  35.4 us (34%)
  waiting for transfers between devices  19.6 us (19%)
  local copies, waits for them, and re-layouts  1.72 us (2%)
  other arithmetic  1.19 us (1%)
    ppermute x4, starting transfers between devices, away(): return lax.ppermute(array, ('key', 'hid_1'), pairs)  14.6 us
    pallas_call x1, Pallas kernels, attend_far(): pl.pallas_call(functools.partial(far_kernel, chunk=chunk, count=count), o...  10.4 us
    pallas_call x1, Pallas kernels, attend_near(): pl.pallas_call(functools.partial(near_kernel, chunk=chunk, count=count),...  8.42 us
    ppermute x3, waiting for transfers between devices, body(): lax.ppermute(merged, 'head_1', shift(4, by))  5.74 us
    ppermute x3, starting transfers between devices, body(): out = out + lax.ppermute(blocks[by - 1], ALONG_X, shift(4, by)).astype(F32)  5.51 us
    ppermute x5, waiting for transfers between devices, swap(): return lax.ppermute(array, axis, shift(2, 1))  4.84 us
    all_to_all x1, starting transfers between devices, body(): new = lax.all_to_all(notes, 'key', split_axis=0, concat_axis=0, tiled=True)  4.59 us
    pallas_call x1, Pallas kernels, first(): pl.pallas_call(first_kernel, out_shape=[shaped((320, 512), BF16), shaped(...  4.55 us
  transfers between devices with their start and end apart: 21, of which 10 were waited for; matrix products, arithmetic and copies ran while one was open for 2% of the time, Pallas kernels for 28%

commit v1 on v0

--- a/solution.py
+++ b/solution.py
@@ -46,7 +46,7 @@
 
 
 SMALL = pl.CostEstimate(flops=1, bytes_accessed=1, transcendentals=0)
-MEDIUM = pl.CostEstimate(flops=2**27, bytes_accessed=2**18, transcendentals=2**10)
+MEDIUM = pl.CostEstimate(flops=2**30, bytes_accessed=2**18, transcendentals=2**10)
 
 
 def shift(n, by):
@@ -641,6 +641,7 @@
     one, keep, pieces = lax.optimization_barrier((one, keep, pieces))
     two = away(one, 1)
     send, keep = second(keep, swap(send, "hid_1"))
+    keep, pieces = lax.optimization_barrier((keep, pieces))
     got = swap(send, "hid_0")
     weights = [pieces[3]]
     for piece, by in zip(pieces, (2, 1, 3)):
@@ -652,9 +653,9 @@
     sign = np.where(np.arange(HD) < middle, -1.0, 1.0).astype(np.float32)
     angles = spots * frequency[None, :]
     cosine, sine = jnp.cos(angles), jnp.sin(angles) * sign[None, :]
-    two, cosine, sine = lax.optimization_barrier((two, cosine, sine))
+    queries, notes = rotated(keep, got, cosine, sine)
+    two, queries = lax.optimization_barrier((two, queries))
     three = away(two, 1)
-    queries, notes = rotated(keep, got, cosine, sine)
     far = swap(queries, "hid_1")
     far, onward = lax.optimization_barrier((far, two[: 2 * HALF]))
     four = away(onward, 2)

time: 103 us -> 98.9 us (0.960); the launches traced: 101 us -> 98.5 us
  waiting for transfers between devices: 19.6 us -> 15.5 us
  Pallas kernels: 35.4 us -> 38.7 us
    pallas_call x1, Pallas kernels: 8.42 us -> 11.7 us  [attend_near(): pl.pallas_call(functools.partial(near_kernel, chunk=chunk, count=count),...]
    ppermute x4, waiting for transfers between devices: 2.85 us -> 0.01 us  [away(): return lax.ppermute(array, ('key', 'hid_1'), pairs)]
    ppermute x3, waiting for transfers between devices: 0.01 us -> 2.7 us  [body(): weights.append(lax.ppermute(piece, 'head_1', shift(4, by)))]
    ppermute x1, starting transfers between devices: 2.74 us -> 0.06 us  [body(): lax.ppermute(across, HID, [(0, 3), (1, 2), (2, 1), (3, 0)])]
    ppermute x4, starting transfers between devices: 14.6 us -> 12.3 us  [away(): return lax.ppermute(array, ('key', 'hid_1'), pairs)]
    ppermute x3, waiting for transfers between devices: 5.74 us -> 3.87 us  [body(): lax.ppermute(merged, 'head_1', shift(4, by))]
    ppermute x3, starting transfers between devices: 4.08 us -> 5.72 us  [body(): lax.ppermute(merged, 'head_1', shift(4, by))]
    all_to_all x1, starting transfers between devices: 4.59 us -> 5.96 us  [body(): new = lax.all_to_all(notes, 'key', split_axis=0, concat_axis=0, tiled=True)]
  transfers between devices with their start and end apart: 21 -> 21, of which waited for: 10 -> 8; matrix products, arithmetic and copies ran while one was open for 2% -> 2% of each run, Pallas kernels for 28% -> 32%
where the time goes in v1:
time: 98.9 us; the launch traced here: 98.5 us
  starting transfers between devices  41.8 us (42%)
  Pallas kernels  38.7 us (39%)
  waiting for transfers between devices  15.5 us (16%)
  other arithmetic  1.19 us (1%)
  local copies, waits for them, and re-layouts  1.09 us (1%)
    ppermute x4, starting transfers between devices, away(): return lax.ppermute(array, ('key', 'hid_1'), pairs)  12.3 us
    pallas_call x1, Pallas kernels, attend_near(): pl.pallas_call(functools.partial(near_kernel, chunk=chunk, count=count),...  11.7 us
    pallas_call x1, Pallas kernels, attend_far(): pl.pallas_call(functools.partial(far_kernel, chunk=chunk, count=count), o...  10.5 us
    all_to_all x1, starting transfers between devices, body(): new = lax.all_to_all(notes, 'key', split_axis=0, concat_axis=0, tiled=True)  5.96 us
    ppermute x3, starting transfers between devices, body(): lax.ppermute(merged, 'head_1', shift(4, by))  5.72 us
    ppermute x3, starting transfers between devices, body(): out = out + lax.ppermute(blocks[by - 1], ALONG_X, shift(4, by)).astype(F32)  5.48 us
    pallas_call x1, Pallas kernels, first(): pl.pallas_call(first_kernel, out_shape=[shaped((320, 512), BF16), shaped(...  4.53 us
    ppermute x3, starting transfers between devices, body(): weights.append(lax.ppermute(piece, 'head_1', shift(4, by)))  4.38 us
  transfers between devices with their start and end apart: 21, of which 8 were waited for; matrix products, arithmetic and copies ran while one was open for 2% of the time, Pallas kernels for 32%

profile of v1, /device:TPU:1, one launch (start us, length us, event | category | flops | bytes accessed | tf_op | source)
XLA Modules:
  0.0 98.5 jit_solution(18347528714093209152)
XLA Ops:
  0.0 3.2 %pack.1 = (bf16[1088,256]{1,0:T(8,128)(2,1)}, f32[256,128]{1,0:T(8,128)}) custom-call(s32[8]{0:T(128)} %places.1, s32[8]{0:T(128)} %slabs.5, bf16[2048,128]{1,0:T(8,128)(2,1)} %bitcast.2, bf16[2048,128]{1,0:T(8,128)(2,1)} %bitcast.3), custom_call_target="tpu_custom_call" | custom-call | flops 1 | bytes 1 | tf_op jit(solution)/shard_map/pack/pallas_call | solution.py:101
  3.2 0.0 copy-start.2
  3.2 0.0 copy-start.3
  3.2 0.0 copy-start.4
  3.2 6.5 %collective-permute-start = (bf16[1088,256]{1,0:T(8,128)(2,1)}, bf16[1088,256]{1,0:T(8,128)(2,1)}, u32[]{:S(2)}, u32[]{:S(2)}) collective-permute-start(bf16[1088,256]{1,0:T(8,128)(2,1)} %get-tuple-element.51.refs_0_), channel_id=1, source_target_pairs={{0,4},{1,29},{4,8},{5,1},{8,12},{9,5},{12,16},{13,9},{16,20},{17,1... | collective-permute-start | bytes 1671176 | tf_op jit(solution)/shard_map/ppermute | solution.py:634
  9.7 4.5 %first.1 = (bf16[320,512]{1,0:T(8,128)(2,1)}, f32[320,512]{1,0:T(8,128)}) custom-call(bf16[256,2048]{1,0:T(8,128)(2,1)} %tokens.1, bf16[2048,1024]{1,0:T(8,128)(2,1)} %query.1, bf16[2048,128]{1,0:T(8,128)(2,1)} %key.1, bf16[2048,128]{1,0:T(8,128)(2,1)} %value.1), custom_call_target="tpu_custom_call" | custom-call | flops 1 | bytes 1 | tf_op jit(solution)/shard_map/first/pallas_call | solution.py:192
  14.3 0.1 collective-permute-start.2
  14.4 3.5 %columns.1 = (bf16[256,2048]{1,0:T(8,128)(2,1)}, bf16[256,2048]{1,0:T(8,128)(2,1)}, bf16[256,2048]{1,0:T(8,128)(2,1)}, bf16[256,2048]{1,0:T(8,128)(2,1)}) custom-call(bf16[256,8192]{1,0:T(8,128)(2,1)} %weight.1), custom_call_target="tpu_custom_call" | custom-call | flops 1 | bytes 1 | tf_op jit(solution)/shard_map/columns/pallas_call | solution.py:133
  17.8 0.0 collective-permute-done.refs_1_
  17.9 1.8 %collective-permute-start.1 = (bf16[1088,256]{1,0:T(8,128)(2,1)}, bf16[1088,256]{1,0:T(8,128)(2,1)}, u32[]{:S(2)}, u32[]{:S(2)}) collective-permute-start(bf16[1088,256]{1,0:T(8,128)(2,1)} %collective-permute-done.refs_1_), channel_id=1, source_target_pairs={{0,4},{1,29},{4,8},{5,1},{8,12},{9,5},{12,16},{13,9},{16,20},{17,1... | collective-permute-start | bytes 1671176 | tf_op jit(solution)/shard_map/ppermute | solution.py:634
  19.6 0.1 second.1
  19.7 1.3 %collective-permute-start.3 = (bf16[288,512]{1,0:T(8,128)(2,1)S(1)}, bf16[288,512]{1,0:T(8,128)(2,1)S(1)}, u32[]{:S(2)}, u32[]{:S(2)}) collective-permute-start(bf16[288,512]{1,0:T(8,128)(2,1)S(1)} %get-tuple-element.66), channel_id=1, source_target_pairs={{0,2},{2,0},{1,3},{3,1},{4,6},{6,4},{5,7},{7,5},{8,10},{10,8},{9,1... | collective-permute-start | bytes 884744 | tf_op jit(solution)/shard_map/ppermute | solution.py:57
  21.0 1.3 %collective-permute-start.10 = (bf16[256,2048]{1,0:T(8,128)(2,1)}, bf16[256,2048]{1,0:T(8,128)(2,1)S(1)}, u32[]{:S(2)}, u32[]{:S(2)}) collective-permute-start(bf16[256,2048]{1,0:T(8,128)(2,1)} %get-tuple-element.82), channel_id=1, source_target_pairs={{0,32},{32,64},{64,96},{96,0},{1,33},{33,65},{65,97},{97,1},{2,34}... | collective-permute-start | bytes 3145736 | tf_op jit(solution)/shard_map/ppermute | solution.py:648
  22.3 1.4 %collective-permute-start.11 = (bf16[256,2048]{1,0:T(8,128)(2,1)}, bf16[256,2048]{1,0:T(8,128)(2,1)S(1)}, u32[]{:S(2)}, u32[]{:S(2)}) collective-permute-start(bf16[256,2048]{1,0:T(8,128)(2,1)} %get-tuple-element.83), channel_id=1, source_target_pairs={{0,96},{32,0},{64,32},{96,64},{1,97},{33,1},{65,33},{97,65},{2,98}... | collective-permute-start | bytes 3145736 | tf_op jit(solution)/shard_map/ppermute | solution.py:648
  23.8 1.6 %collective-permute-start.9 = (bf16[256,2048]{1,0:T(8,128)(2,1)}, bf16[256,2048]{1,0:T(8,128)(2,1)}, u32[]{:S(2)}, u32[]{:S(2)}) collective-permute-start(bf16[256,2048]{1,0:T(8,128)(2,1)} %get-tuple-element.81), channel_id=1, source_target_pairs={{0,64},{32,96},{64,0},{96,32},{1,65},{33,97},{65,1},{97,33},{2,66}... | collective-permute-start | bytes 3145736 | tf_op jit(solution)/shard_map/ppermute | solution.py:648
  25.4 0.5 sine_multiply_fusion
  25.9 2.4 %collective-permute-done.3.got = bf16[288,512]{1,0:T(8,128)(2,1)S(1)} collective-permute-done((bf16[288,512]{1,0:T(8,128)(2,1)S(1)}, bf16[288,512]{1,0:T(8,128)(2,1)S(1)}, u32[]{:S(2)}, u32[]{:S(2)}) %collective-permute-start.3) | collective-permute-done | bytes 294944 | tf_op jit(solution)/shard_map/ppermute | solution.py:57
  28.3 1.0 %rotated.1 = (bf16[256,512]{1,0:T(8,128)(2,1)}, bf16[8,64,256]{2,1,0:T(8,128)(2,1)}) custom-call(f32[288,512]{1,0:T(8,128)S(1)} %get-tuple-element.65.keep, bf16[288,512]{1,0:T(8,128)(2,1)S(1)} %collective-permute-done.3.got, f32[256,128]{1,0:T(8,128)S(1)} %get-tuple-element.98.cosine, f32[256,128]{1,0:T(8,128)S(1)} %get-tuple-element.97.sine), custom_call_target="tpu_custom_call" | custom-call | flops 1 | bytes 1 | tf_op jit(solution)/shard_map/rotated/pallas_call | solution.py:258
  29.3 0.4 collective-permute-start.5
  29.7 0.0 collective-permute-start.4
  29.7 6.0 %all-to-all-start = ((bf16[8,64,256]{2,1,0:T(8,128)(2,1)}), bf16[8,64,256]{2,1,0:T(8,128)(2,1)}, u32[]{:S(2)}, u32[]{:S(2)}) async-start(bf16[8,64,256]{2,1,0:T(8,128)(2,1)} %get-tuple-element.72.notes), calls=%async_computation | async-start | bytes 524288 | tf_op jit(solution)/shard_map/all_to_all | solution.py:663
  35.7 1.1 %slice.3 = bf16[544,256]{1,0:T(8,128)(2,1)S(1)} slice(bf16[1088,256]{1,0:T(8,128)(2,1)} %collective-permute-done.1.refs_2_), slice={[0:544], [0:256]} | slice | bytes 557056 | tf_op jit(solution)/shard_map/slice | solution.py:660
  36.8 3.6 %collective-permute-start.6 = (bf16[544,256]{1,0:T(8,128)(2,1)S(1)}, bf16[544,256]{1,0:T(8,128)(2,1)}, u32[]{:S(2)}, u32[]{:S(2)}) collective-permute-start(bf16[544,256]{1,0:T(8,128)(2,1)S(1)} %slice.3), channel_id=1, source_target_pairs={{0,8},{1,25},{4,12},{5,29},{8,16},{9,1},{12,20},{13,5},{16,24},{17... | collective-permute-start | bytes 835592 | tf_op jit(solution)/shard_map/ppermute | solution.py:634
  40.4 11.7 %near.1 = (bf16[2048,128]{1,0:T(8,128)(2,1)}, f32[2048,128]{1,0:T(8,128)}, f32[2048,128]{1,0:T(8,128)}) custom-call(s32[8]{0:T(128)} %slabs.5, bf16[256,512]{1,0:T(8,128)(2,1)} %get-tuple-element.69.near, bf16[256,512]{1,0:T(8,128)(2,1)} %collective-permute-done.4.far, bf16[8,64,256]{2,1,0:T(8,128)(2,1)} %get-tuple-element.72.notes, ...), custom_call_target="tpu_custom_call" | custom-call | flops 1 | bytes 1 | tf_op jit(solution)/shard_map/near/pallas_call | solution.py:425
  52.2 0.0 all-to-all-done.refs_3_
  52.2 10.5 %far.1 = (bf16[2,272,256]{2,1,0:T(8,128)(2,1)}, bf16[272,256]{1,0:T(8,128)(2,1)}, bf16[272,256]{1,0:T(8,128)(2,1)}) custom-call(s32[8]{0:T(128)} %slabs.5, bf16[2048,128]{1,0:T(8,128)(2,1)} %get-tuple-element.73.refs_0_, f32[2048,128]{1,0:T(8,128)} %get-tuple-element.74.refs_1_, f32[2048,128]{1,0:T(8,128)} %get-tuple-element.75.refs_2_, ...), custom_call_target="tpu_custom_call" | custom-call | flops 1073741824 | bytes 262144 | tf_op jit(solution)/shard_map/far/pallas_call | solution.py:509
  62.7 1.3 %collective-permute-start.7 = (bf16[272,256]{1,0:T(8,128)(2,1)}, bf16[272,256]{1,0:T(8,128)(2,1)}, u32[]{:S(2)}, u32[]{:S(2)}) collective-permute-start(bf16[272,256]{1,0:T(8,128)(2,1)} %get-tuple-element.78), channel_id=1, source_target_pairs={{0,2},{2,0},{1,3},{3,1},{4,6},{6,4},{5,7},{7,5},{8,10},{10,8},{9,1... | collective-permute-start | bytes 417800 | tf_op jit(solution)/shard_map/ppermute | solution.py:57
  64.0 0.1 collective-permute-start.8
  64.0 4.0 %all-to-all-start.1 = ((bf16[2,272,256]{2,1,0:T(8,128)(2,1)}), bf16[2,272,256]{2,1,0:T(8,128)(2,1)S(1)}, u32[]{:S(2)}, u32[]{:S(2)}) async-start(bf16[2,272,256]{2,1,0:T(8,128)(2,1)} %get-tuple-element.77), calls=%async_computation.1 | async-start | bytes 557056 | tf_op jit(solution)/shard_map/all_to_all | solution.py:668
  68.1 2.7 %collective-permute-done.9.refs_5_ = bf16[256,2048]{1,0:T(8,128)(2,1)} collective-permute-done((bf16[256,2048]{1,0:T(8,128)(2,1)}, bf16[256,2048]{1,0:T(8,128)(2,1)}, u32[]{:S(2)}, u32[]{:S(2)}) %collective-permute-start.9) | collective-permute-done | bytes 1048608 | tf_op jit(solution)/shard_map/ppermute | solution.py:648
  70.8 0.0 all-to-all-done.1.pair
  70.8 0.9 collective-permute-done.8.across
  71.7 1.5 %merge.1.refs_0_ = bf16[256,256]{1,0:T(8,128)(2,1)S(1)} custom-call(bf16[2,272,256]{2,1,0:T(8,128)(2,1)S(1)} %all-to-all-done.1.pair, bf16[272,256]{1,0:T(8,128)(2,1)} %collective-permute-done.7.straight, bf16[272,256]{1,0:T(8,128)(2,1)} %collective-permute-done.8.across), custom_call_target="tpu_custom_call" | custom-call | flops 1 | bytes 1 | tf_op jit(solution)/shard_map/merge/pallas_call | solution.py:554
  73.2 3.0 %collective-permute-start.12 = (bf16[256,256]{1,0:T(8,128)(2,1)S(1)}, bf16[256,256]{1,0:T(8,128)(2,1)S(1)}, u32[]{:S(2)}, u32[]{:S(2)}) collective-permute-start(bf16[256,256]{1,0:T(8,128)(2,1)S(1)} %merge.1.refs_0_), channel_id=1, source_target_pairs={{0,64},{32,96},{64,0},{96,32},{1,65},{33,97},{65,1},{97,33},{2,66}... | collective-permute-start | bytes 393224 | tf_op jit(solution)/shard_map/ppermute | solution.py:675
  76.2 0.4 collective-permute-start.13
  76.6 2.3 %collective-permute-start.14 = (bf16[256,256]{1,0:T(8,128)(2,1)S(1)}, bf16[256,256]{1,0:T(8,128)(2,1)S(1)}, u32[]{:S(2)}, u32[]{:S(2)}) collective-permute-start(bf16[256,256]{1,0:T(8,128)(2,1)S(1)} %merge.1.refs_0_), channel_id=1, source_target_pairs={{0,96},{32,0},{64,32},{96,64},{1,97},{33,1},{65,33},{97,65},{2,98}... | collective-permute-start | bytes 393224 | tf_op jit(solution)/shard_map/ppermute | solution.py:675
  78.9 0.5 collective-permute-done.12.refs_1_
  79.5 3.3 %collective-permute-done.13.refs_2_ = bf16[256,256]{1,0:T(8,128)(2,1)S(1)} collective-permute-done((bf16[256,256]{1,0:T(8,128)(2,1)S(1)}, bf16[256,256]{1,0:T(8,128)(2,1)S(1)}, u32[]{:S(2)}, u32[]{:S(2)}) %collective-permute-start.13) | collective-permute-done | bytes 131104 | tf_op jit(solution)/shard_map/ppermute | solution.py:675
  82.8 2.5 %project.1 = (bf16[256,1024]{1,0:T(8,128)(2,1)S(1)}, f32[256,1024]{1,0:T(8,128)S(1)}) custom-call(bf16[256,256]{1,0:T(8,128)(2,1)S(1)} %merge.1.refs_0_, bf16[256,256]{1,0:T(8,128)(2,1)S(1)} %collective-permute-done.12.refs_1_, bf16[256,256]{1,0:T(8,128)(2,1)S(1)} %collective-permute-done.13.refs_2_, bf16[256,256]{1,0:T(8,128)(2,1)S(1)} %collective-permute-done.14.refs_3_, ...), custom_call_target="tpu_custom_call" | custom-call | flops 1 | bytes 1 | tf_op jit(solution)/shard_map/project/pallas_call | solution.py:579
  85.3 1.2 %collective-permute-start.15 = (bf16[256,1024]{1,0:T(8,128)(2,1)S(1)}, bf16[256,1024]{1,0:T(8,128)(2,1)S(1)}, u32[]{:S(2)}, u32[]{:S(2)}) collective-permute-start(bf16[256,1024]{1,0:T(8,128)(2,1)S(1)} %get-tuple-element.92), channel_id=1, source_target_pairs={{0,1},{1,0},{2,3},{3,2},{4,5},{5,4},{6,7},{7,6},{8,9},{9,8},{10,11... | collective-permute-start | bytes 1572872 | tf_op jit(solution)/shard_map/ppermute | solution.py:57
  86.5 1.5 %collective-permute-done.15.got = bf16[256,1024]{1,0:T(8,128)(2,1)S(1)} collective-permute-done((bf16[256,1024]{1,0:T(8,128)(2,1)S(1)}, bf16[256,1024]{1,0:T(8,128)(2,1)S(1)}, u32[]{:S(2)}, u32[]{:S(2)}) %collective-permute-start.15) | collective-permute-done | bytes 524320 | tf_op jit(solution)/shard_map/ppermute | solution.py:57
  88.0 0.1 split.1
  88.2 2.8 %collective-permute-start.16 = (bf16[256,256]{1,0:T(8,128)(2,1)S(1)}, bf16[256,256]{1,0:T(8,128)(2,1)S(1)}, u32[]{:S(2)}, u32[]{:S(2)}) collective-permute-start(bf16[256,256]{1,0:T(8,128)(2,1)S(1)} %get-tuple-element.94), channel_id=1, source_target_pairs={{0,128},{2,130},{128,0},{130,2},{1,129},{3,131},{129,1},{131,3},{4... | collective-permute-start | bytes 393224 | tf_op jit(solution)/shard_map/ppermute | solution.py:680
  91.0 0.3 collective-permute-start.17
  91.3 2.3 %collective-permute-start.18 = (bf16[256,256]{1,0:T(8,128)(2,1)S(1)}, bf16[256,256]{1,0:T(8,128)(2,1)S(1)}, u32[]{:S(2)}, u32[]{:S(2)}) collective-permute-start(bf16[256,256]{1,0:T(8,128)(2,1)S(1)} %get-tuple-element.96), channel_id=1, source_target_pairs={{0,130},{2,0},{128,2},{130,128},{1,131},{3,1},{129,3},{131,129},{4... | collective-permute-start | bytes 393224 | tf_op jit(solution)/shard_map/ppermute | solution.py:680
  93.7 0.8 collective-permute-done.16
  94.5 3.3 %collective-permute-done.17 = bf16[256,256]{1,0:T(8,128)(2,1)S(1)} collective-permute-done((bf16[256,256]{1,0:T(8,128)(2,1)S(1)}, bf16[256,256]{1,0:T(8,128)(2,1)S(1)}, u32[]{:S(2)}, u32[]{:S(2)}) %collective-permute-start.17) | collective-permute-done | bytes 131104 | tf_op jit(solution)/shard_map/ppermute | solution.py:680
  97.8 0.7 add_convert_fusion
  (17 shorter events, 0.0 us)
Async XLA Ops:
  3.2 22.2 %copy-start.2 = (f32[256,128]{1,0:T(8,128)S(1)}, f32[256,128]{1,0:T(8,128)}, u32[]{:S(2)}) copy-start(f32[256,128]{1,0:T(8,128)} %get-tuple-element.67) | copy-start | bytes 393220
  3.2 22.2 %copy-start.3 = (f32[128]{0:T(128)S(1)}, f32[128]{0:T(128)}, u32[]{:S(2)}) copy-start(f32[128]{0:T(128)} %constant.11) | copy-start | bytes 1540
  3.2 22.2 %copy-start.4 = (f32[128]{0:T(128)S(1)}, f32[128]{0:T(128)}, u32[]{:S(2)}) copy-start(f32[128]{0:T(128)} %constant.12) | copy-start | bytes 1540
  3.2 14.6 %collective-permute-start = (bf16[1088,256]{1,0:T(8,128)(2,1)}, bf16[1088,256]{1,0:T(8,128)(2,1)}, u32[]{:S(2)}, u32[]{:S(2)}) collective-permute-start(bf16[1088,256]{1,0:T(8,128)(2,1)} %get-tuple-element.51.refs_0_), channel_id=1, source_target_pairs={{0,4},{1,29},{4,8},{5,1},{8,12},{9,5},{12,16},{13,9},{16,20},{17,1... | collective-permute-start | bytes 1671176 | tf_op jit(solution)/shard_map/ppermute | solution.py:634
  14.3 5.4 %copy-start.1 = (f32[320,512]{1,0:T(8,128)S(1)}, f32[320,512]{1,0:T(8,128)}, u32[]{:S(2)}) copy-start(f32[320,512]{1,0:T(8,128)} %get-tuple-element.58.keep) | copy-start | bytes 1966084
  14.3 5.4 %collective-permute-start.2 = (bf16[320,512]{1,0:T(8,128)(2,1)}, bf16[320,512]{1,0:T(8,128)(2,1)S(1)}, u32[]{:S(2)}, u32[]{:S(2)}) collective-permute-start(bf16[320,512]{1,0:T(8,128)(2,1)} %get-tuple-element.59), channel_id=1, source_target_pairs={{0,1},{1,0},{2,3},{3,2},{4,5},{5,4},{6,7},{7,6},{8,9},{9,8},{10,11... | collective-permute-start | bytes 983048 | tf_op jit(solution)/shard_map/ppermute | solution.py:57
  17.9 11.5 %collective-permute-start.1 = (bf16[1088,256]{1,0:T(8,128)(2,1)}, bf16[1088,256]{1,0:T(8,128)(2,1)}, u32[]{:S(2)}, u32[]{:S(2)}) collective-permute-start(bf16[1088,256]{1,0:T(8,128)(2,1)} %collective-permute-done.refs_1_), channel_id=1, source_target_pairs={{0,4},{1,29},{4,8},{5,1},{8,12},{9,5},{12,16},{13,9},{16,20},{17,1... | collective-permute-start | bytes 1671176 | tf_op jit(solution)/shard_map/ppermute | solution.py:634
  19.7 8.6 %collective-permute-start.3 = (bf16[288,512]{1,0:T(8,128)(2,1)S(1)}, bf16[288,512]{1,0:T(8,128)(2,1)S(1)}, u32[]{:S(2)}, u32[]{:S(2)}) collective-permute-start(bf16[288,512]{1,0:T(8,128)(2,1)S(1)} %get-tuple-element.66), channel_id=1, source_target_pairs={{0,2},{2,0},{1,3},{3,1},{4,6},{6,4},{5,7},{7,5},{8,10},{10,8},{9,1... | collective-permute-start | bytes 884744 | tf_op jit(solution)/shard_map/ppermute | solution.py:57
  21.0 47.1 %collective-permute-start.10 = (bf16[256,2048]{1,0:T(8,128)(2,1)}, bf16[256,2048]{1,0:T(8,128)(2,1)S(1)}, u32[]{:S(2)}, u32[]{:S(2)}) collective-permute-start(bf16[256,2048]{1,0:T(8,128)(2,1)} %get-tuple-element.82), channel_id=1, source_target_pairs={{0,32},{32,64},{64,96},{96,0},{1,33},{33,65},{65,97},{97,1},{2,34}... | collective-permute-start | bytes 3145736 | tf_op jit(solution)/shard_map/ppermute | solution.py:648
  22.3 45.8 %collective-permute-start.11 = (bf16[256,2048]{1,0:T(8,128)(2,1)}, bf16[256,2048]{1,0:T(8,128)(2,1)S(1)}, u32[]{:S(2)}, u32[]{:S(2)}) collective-permute-start(bf16[256,2048]{1,0:T(8,128)(2,1)} %get-tuple-element.83), channel_id=1, source_target_pairs={{0,96},{32,0},{64,32},{96,64},{1,97},{33,1},{65,33},{97,65},{2,98}... | collective-permute-start | bytes 3145736 | tf_op jit(solution)/shard_map/ppermute | solution.py:648
  23.8 47.0 %collective-permute-start.9 = (bf16[256,2048]{1,0:T(8,128)(2,1)}, bf16[256,2048]{1,0:T(8,128)(2,1)}, u32[]{:S(2)}, u32[]{:S(2)}) collective-permute-start(bf16[256,2048]{1,0:T(8,128)(2,1)} %get-tuple-element.81), channel_id=1, source_target_pairs={{0,64},{32,96},{64,0},{96,32},{1,65},{33,97},{65,1},{97,33},{2,66}... | collective-permute-start | bytes 3145736 | tf_op jit(solution)/shard_map/ppermute | solution.py:648
  29.3 22.9 %collective-permute-start.5 = (bf16[1088,256]{1,0:T(8,128)(2,1)}, bf16[1088,256]{1,0:T(8,128)(2,1)}, u32[]{:S(2)}, u32[]{:S(2)}) collective-permute-start(bf16[1088,256]{1,0:T(8,128)(2,1)} %collective-permute-done.1.refs_2_), channel_id=1, source_target_pairs={{0,4},{1,29},{4,8},{5,1},{8,12},{9,5},{12,16},{13,9},{16,20},{17,1... | collective-permute-start | bytes 1671176 | tf_op jit(solution)/shard_map/ppermute | solution.py:634
  29.7 7.0 %collective-permute-start.4 = (bf16[256,512]{1,0:T(8,128)(2,1)}, bf16[256,512]{1,0:T(8,128)(2,1)}, u32[]{:S(2)}, u32[]{:S(2)}) collective-permute-start(bf16[256,512]{1,0:T(8,128)(2,1)} %get-tuple-element.69.near), channel_id=1, source_target_pairs={{0,1},{1,0},{2,3},{3,2},{4,5},{5,4},{6,7},{7,6},{8,9},{9,8},{10,11... | collective-permute-start | bytes 786440 | tf_op jit(solution)/shard_map/ppermute | solution.py:57
  29.7 22.4 %all-to-all-start = ((bf16[8,64,256]{2,1,0:T(8,128)(2,1)}), bf16[8,64,256]{2,1,0:T(8,128)(2,1)}, u32[]{:S(2)}, u32[]{:S(2)}) async-start(bf16[8,64,256]{2,1,0:T(8,128)(2,1)} %get-tuple-element.72.notes), calls=%async_computation | async-start | bytes 524288 | tf_op jit(solution)/shard_map/all_to_all | solution.py:663
  35.7 47.1 %copy-start = (bf16[256,2048]{1,0:T(8,128)(2,1)S(1)}, bf16[256,2048]{1,0:T(8,128)(2,1)}, u32[]{:S(2)}) copy-start(bf16[256,2048]{1,0:T(8,128)(2,1)} %get-tuple-element.87.refs_4_) | copy-start | bytes 3145732
  36.8 15.4 %collective-permute-start.6 = (bf16[544,256]{1,0:T(8,128)(2,1)S(1)}, bf16[544,256]{1,0:T(8,128)(2,1)}, u32[]{:S(2)}, u32[]{:S(2)}) collective-permute-start(bf16[544,256]{1,0:T(8,128)(2,1)S(1)} %slice.3), channel_id=1, source_target_pairs={{0,8},{1,25},{4,12},{5,29},{8,16},{9,1},{12,20},{13,5},{16,24},{17... | collective-permute-start | bytes 835592 | tf_op jit(solution)/shard_map/ppermute | solution.py:634
  62.7 8.1 %collective-permute-start.7 = (bf16[272,256]{1,0:T(8,128)(2,1)}, bf16[272,256]{1,0:T(8,128)(2,1)}, u32[]{:S(2)}, u32[]{:S(2)}) collective-permute-start(bf16[272,256]{1,0:T(8,128)(2,1)} %get-tuple-element.78), channel_id=1, source_target_pairs={{0,2},{2,0},{1,3},{3,1},{4,6},{6,4},{5,7},{7,5},{8,10},{10,8},{9,1... | collective-permute-start | bytes 417800 | tf_op jit(solution)/shard_map/ppermute | solution.py:57
  64.0 7.7 %collective-permute-start.8 = (bf16[272,256]{1,0:T(8,128)(2,1)}, bf16[272,256]{1,0:T(8,128)(2,1)}, u32[]{:S(2)}, u32[]{:S(2)}) collective-permute-start(bf16[272,256]{1,0:T(8,128)(2,1)} %get-tuple-element.79), channel_id=1, source_target_pairs={{0,3},{1,2},{2,1},{3,0},{4,7},{5,6},{6,5},{7,4},{8,11},{9,10},{10,... | collective-permute-start | bytes 417800 | tf_op jit(solution)/shard_map/ppermute | solution.py:670
  64.0 6.7 %all-to-all-start.1 = ((bf16[2,272,256]{2,1,0:T(8,128)(2,1)}), bf16[2,272,256]{2,1,0:T(8,128)(2,1)S(1)}, u32[]{:S(2)}, u32[]{:S(2)}) async-start(bf16[2,272,256]{2,1,0:T(8,128)(2,1)} %get-tuple-element.77), calls=%async_computation.1 | async-start | bytes 557056 | tf_op jit(solution)/shard_map/all_to_all | solution.py:668
  73.2 6.3 %collective-permute-start.12 = (bf16[256,256]{1,0:T(8,128)(2,1)S(1)}, bf16[256,256]{1,0:T(8,128)(2,1)S(1)}, u32[]{:S(2)}, u32[]{:S(2)}) collective-permute-start(bf16[256,256]{1,0:T(8,128)(2,1)S(1)} %merge.1.refs_0_), channel_id=1, source_target_pairs={{0,64},{32,96},{64,0},{96,32},{1,65},{33,97},{65,1},{97,33},{2,66}... | collective-permute-start | bytes 393224 | tf_op jit(solution)/shard_map/ppermute | solution.py:675
  76.2 6.5 %collective-permute-start.13 = (bf16[256,256]{1,0:T(8,128)(2,1)S(1)}, bf16[256,256]{1,0:T(8,128)(2,1)S(1)}, u32[]{:S(2)}, u32[]{:S(2)}) collective-permute-start(bf16[256,256]{1,0:T(8,128)(2,1)S(1)} %merge.1.refs_0_), channel_id=1, source_target_pairs={{0,32},{32,64},{64,96},{96,0},{1,33},{33,65},{65,97},{97,1},{2,34}... | collective-permute-start | bytes 393224 | tf_op jit(solution)/shard_map/ppermute | solution.py:675
  76.6 6.2 %collective-permute-start.14 = (bf16[256,256]{1,0:T(8,128)(2,1)S(1)}, bf16[256,256]{1,0:T(8,128)(2,1)S(1)}, u32[]{:S(2)}, u32[]{:S(2)}) collective-permute-start(bf16[256,256]{1,0:T(8,128)(2,1)S(1)} %merge.1.refs_0_), channel_id=1, source_target_pairs={{0,96},{32,0},{64,32},{96,64},{1,97},{33,1},{65,33},{97,65},{2,98}... | collective-permute-start | bytes 393224 | tf_op jit(solution)/shard_map/ppermute | solution.py:675
  85.3 2.7 %collective-permute-start.15 = (bf16[256,1024]{1,0:T(8,128)(2,1)S(1)}, bf16[256,1024]{1,0:T(8,128)(2,1)S(1)}, u32[]{:S(2)}, u32[]{:S(2)}) collective-permute-start(bf16[256,1024]{1,0:T(8,128)(2,1)S(1)} %get-tuple-element.92), channel_id=1, source_target_pairs={{0,1},{1,0},{2,3},{3,2},{4,5},{5,4},{6,7},{7,6},{8,9},{9,8},{10,11... | collective-permute-start | bytes 1572872 | tf_op jit(solution)/shard_map/ppermute | solution.py:57
  88.2 6.3 %collective-permute-start.16 = (bf16[256,256]{1,0:T(8,128)(2,1)S(1)}, bf16[256,256]{1,0:T(8,128)(2,1)S(1)}, u32[]{:S(2)}, u32[]{:S(2)}) collective-permute-start(bf16[256,256]{1,0:T(8,128)(2,1)S(1)} %get-tuple-element.94), channel_id=1, source_target_pairs={{0,128},{2,130},{128,0},{130,2},{1,129},{3,131},{129,1},{131,3},{4... | collective-permute-start | bytes 393224 | tf_op jit(solution)/shard_map/ppermute | solution.py:680
  91.0 6.8 %collective-permute-start.17 = (bf16[256,256]{1,0:T(8,128)(2,1)S(1)}, bf16[256,256]{1,0:T(8,128)(2,1)S(1)}, u32[]{:S(2)}, u32[]{:S(2)}) collective-permute-start(bf16[256,256]{1,0:T(8,128)(2,1)S(1)} %get-tuple-element.95), channel_id=1, source_target_pairs={{0,2},{2,128},{128,130},{130,0},{1,3},{3,129},{129,131},{131,1},{4... | collective-permute-start | bytes 393224 | tf_op jit(solution)/shard_map/ppermute | solution.py:680
  91.3 6.4 %collective-permute-start.18 = (bf16[256,256]{1,0:T(8,128)(2,1)S(1)}, bf16[256,256]{1,0:T(8,128)(2,1)S(1)}, u32[]{:S(2)}, u32[]{:S(2)}) collective-permute-start(bf16[256,256]{1,0:T(8,128)(2,1)S(1)} %get-tuple-element.96), channel_id=1, source_target_pairs={{0,130},{2,0},{128,2},{130,128},{1,131},{3,1},{129,3},{131,129},{4... | collective-permute-start | bytes 393224 | tf_op jit(solution)/shard_map/ppermute | solution.py:680

commit v2 on v1

--- a/solution.py
+++ b/solution.py
@@ -669,7 +669,7 @@
         swap(straight, "hid_0"),
         lax.ppermute(across, HID, [(0, 3), (1, 2), (2, 1), (3, 0)]),
     ]
-    parts, weights = lax.optimization_barrier((parts, weights))
+    parts, weights[2:] = lax.optimization_barrier((parts, weights[2:]))
     merged = merge(parts)
 
     heads = [merged] + [lax.ppermute(merged, "head_1", shift(4, by)) for by in (2, 1, 3)]

time: 98.9 us -> 99.3 us (level)
  waiting for transfers between devices: 15.5 us -> 17.3 us
  starting transfers between devices: 41.8 us -> 40.5 us
    ppermute x3, waiting for transfers between devices: 2.7 us -> 4.5 us  [body(): weights.append(lax.ppermute(piece, 'head_1', shift(4, by)))]
  transfers between devices with their start and end apart: 21 -> 21, of which waited for: 8 -> 8; matrix products, arithmetic and copies ran while one was open for 2% -> 2% of each run, Pallas kernels for 32% -> 33%
where the time goes in v2:
time: 99.3 us; the launch traced here: 98.9 us
  starting transfers between devices  40.5 us (41%)
  Pallas kernels  38.8 us (39%)
  waiting for transfers between devices  17.3 us (17%)
  other arithmetic  1.19 us (1%)
  local copies, waits for them, and re-layouts  1.09 us (1%)
    ppermute x4, starting transfers between devices, away(): return lax.ppermute(array, ('key', 'hid_1'), pairs)  12.1 us
    pallas_call x1, Pallas kernels, attend_near(): pl.pallas_call(functools.partial(near_kernel, chunk=chunk, count=count),...  11.8 us
    pallas_call x1, Pallas kernels, attend_far(): pl.pallas_call(functools.partial(far_kernel, chunk=chunk, count=count), o...  10.5 us
    all_to_all x1, starting transfers between devices, body(): new = lax.all_to_all(notes, 'key', split_axis=0, concat_axis=0, tiled=True)  6.12 us
    ppermute x3, starting transfers between devices, body(): out = out + lax.ppermute(blocks[by - 1], ALONG_X, shift(4, by)).astype(F32)  5.23 us
    ppermute x3, starting transfers between devices, body(): lax.ppermute(merged, 'head_1', shift(4, by))  4.83 us
    ppermute x3, waiting for transfers between devices, body(): lax.ppermute(merged, 'head_1', shift(4, by))  4.6 us
    pallas_call x1, Pallas kernels, first(): pl.pallas_call(first_kernel, out_shape=[shaped((320, 512), BF16), shaped(...  4.54 us
  transfers between devices with their start and end apart: 21, of which 8 were waited for; matrix products, arithmetic and copies ran while one was open for 2% of the time, Pallas kernels for 33%

profile of v2, /device:TPU:1, one launch (start us, length us, event | category | flops | bytes accessed | tf_op | source)
XLA Modules:
  0.0 98.9 jit_solution(16971257900697734928)
XLA Ops:
  0.0 3.2 %pack.1 = (bf16[1088,256]{1,0:T(8,128)(2,1)}, f32[256,128]{1,0:T(8,128)}) custom-call(s32[8]{0:T(128)} %places.1, s32[8]{0:T(128)} %slabs.5, bf16[2048,128]{1,0:T(8,128)(2,1)} %bitcast.2, bf16[2048,128]{1,0:T(8,128)(2,1)} %bitcast.3), custom_call_target="tpu_custom_call" | custom-call | flops 1 | bytes 1 | tf_op jit(solution)/shard_map/pack/pallas_call | solution.py:101
  3.2 0.0 copy-start.2
  3.2 0.0 copy-start.3
  3.2 0.0 copy-start.4
  3.2 6.5 %collective-permute-start = (bf16[1088,256]{1,0:T(8,128)(2,1)}, bf16[1088,256]{1,0:T(8,128)(2,1)}, u32[]{:S(2)}, u32[]{:S(2)}) collective-permute-start(bf16[1088,256]{1,0:T(8,128)(2,1)} %get-tuple-element.49.refs_0_), channel_id=1, source_target_pairs={{0,4},{1,29},{4,8},{5,1},{8,12},{9,5},{12,16},{13,9},{16,20},{17,1... | collective-permute-start | bytes 1671176 | tf_op jit(solution)/shard_map/ppermute | solution.py:634
  9.7 4.5 %first.1 = (bf16[320,512]{1,0:T(8,128)(2,1)}, f32[320,512]{1,0:T(8,128)}) custom-call(bf16[256,2048]{1,0:T(8,128)(2,1)} %tokens.1, bf16[2048,1024]{1,0:T(8,128)(2,1)} %query.1, bf16[2048,128]{1,0:T(8,128)(2,1)} %key.1, bf16[2048,128]{1,0:T(8,128)(2,1)} %value.1), custom_call_target="tpu_custom_call" | custom-call | flops 1 | bytes 1 | tf_op jit(solution)/shard_map/first/pallas_call | solution.py:192
  14.3 0.1 collective-permute-start.2
  14.4 3.5 %columns.1 = (bf16[256,2048]{1,0:T(8,128)(2,1)}, bf16[256,2048]{1,0:T(8,128)(2,1)}, bf16[256,2048]{1,0:T(8,128)(2,1)}, bf16[256,2048]{1,0:T(8,128)(2,1)}) custom-call(bf16[256,8192]{1,0:T(8,128)(2,1)} %weight.1), custom_call_target="tpu_custom_call" | custom-call | flops 1 | bytes 1 | tf_op jit(solution)/shard_map/columns/pallas_call | solution.py:133
  17.8 0.0 collective-permute-done.refs_1_
  17.9 1.8 %collective-permute-start.1 = (bf16[1088,256]{1,0:T(8,128)(2,1)}, bf16[1088,256]{1,0:T(8,128)(2,1)}, u32[]{:S(2)}, u32[]{:S(2)}) collective-permute-start(bf16[1088,256]{1,0:T(8,128)(2,1)} %collective-permute-done.refs_1_), channel_id=1, source_target_pairs={{0,4},{1,29},{4,8},{5,1},{8,12},{9,5},{12,16},{13,9},{16,20},{17,1... | collective-permute-start | bytes 1671176 | tf_op jit(solution)/shard_map/ppermute | solution.py:634
  19.6 0.0 collective-permute-done.2.got
  19.6 0.1 second.1
  19.7 1.3 %collective-permute-start.3 = (bf16[288,512]{1,0:T(8,128)(2,1)S(1)}, bf16[288,512]{1,0:T(8,128)(2,1)S(1)}, u32[]{:S(2)}, u32[]{:S(2)}) collective-permute-start(bf16[288,512]{1,0:T(8,128)(2,1)S(1)} %get-tuple-element.64), channel_id=1, source_target_pairs={{0,2},{2,0},{1,3},{3,1},{4,6},{6,4},{5,7},{7,5},{8,10},{10,8},{9,1... | collective-permute-start | bytes 884744 | tf_op jit(solution)/shard_map/ppermute | solution.py:57
  21.0 2.7 %collective-permute-start.10 = (bf16[256,2048]{1,0:T(8,128)(2,1)}, bf16[256,2048]{1,0:T(8,128)(2,1)S(1)}, u32[]{:S(2)}, u32[]{:S(2)}) collective-permute-start(bf16[256,2048]{1,0:T(8,128)(2,1)} %get-tuple-element.79), channel_id=1, source_target_pairs={{0,96},{32,0},{64,32},{96,64},{1,97},{33,1},{65,33},{97,65},{2,98}... | collective-permute-start | bytes 3145736 | tf_op jit(solution)/shard_map/ppermute | solution.py:648
  23.8 1.6 %collective-permute-start.14 = (bf16[256,2048]{1,0:T(8,128)(2,1)}, bf16[256,2048]{1,0:T(8,128)(2,1)}, u32[]{:S(2)}, u32[]{:S(2)}) collective-permute-start(bf16[256,2048]{1,0:T(8,128)(2,1)} %get-tuple-element.84), channel_id=1, source_target_pairs={{0,64},{32,96},{64,0},{96,32},{1,65},{33,97},{65,1},{97,33},{2,66}... | collective-permute-start | bytes 3145736 | tf_op jit(solution)/shard_map/ppermute | solution.py:648
  25.4 0.5 sine_multiply_fusion
  25.9 2.4 %collective-permute-done.3.got = bf16[288,512]{1,0:T(8,128)(2,1)S(1)} collective-permute-done((bf16[288,512]{1,0:T(8,128)(2,1)S(1)}, bf16[288,512]{1,0:T(8,128)(2,1)S(1)}, u32[]{:S(2)}, u32[]{:S(2)}) %collective-permute-start.3) | collective-permute-done | bytes 294944 | tf_op jit(solution)/shard_map/ppermute | solution.py:57
  28.3 1.0 %rotated.1 = (bf16[256,512]{1,0:T(8,128)(2,1)}, bf16[8,64,256]{2,1,0:T(8,128)(2,1)}) custom-call(f32[288,512]{1,0:T(8,128)S(1)} %get-tuple-element.63.keep, bf16[288,512]{1,0:T(8,128)(2,1)S(1)} %collective-permute-done.3.got, f32[256,128]{1,0:T(8,128)S(1)} %get-tuple-element.94.cosine, f32[256,128]{1,0:T(8,128)S(1)} %get-tuple-element.93.sine), custom_call_target="tpu_custom_call" | custom-call | flops 1 | bytes 1 | tf_op jit(solution)/shard_map/rotated/pallas_call | solution.py:258
  29.3 0.0 collective-permute-done.1.refs_2_
  29.3 0.2 collective-permute-start.5
  29.5 0.0 collective-permute-start.4
  29.6 6.1 %all-to-all-start = ((bf16[8,64,256]{2,1,0:T(8,128)(2,1)}), bf16[8,64,256]{2,1,0:T(8,128)(2,1)}, u32[]{:S(2)}, u32[]{:S(2)}) async-start(bf16[8,64,256]{2,1,0:T(8,128)(2,1)} %get-tuple-element.70.notes), calls=%async_computation | async-start | bytes 524288 | tf_op jit(solution)/shard_map/all_to_all | solution.py:663
  35.7 1.1 %slice.3 = bf16[544,256]{1,0:T(8,128)(2,1)S(1)} slice(bf16[1088,256]{1,0:T(8,128)(2,1)} %collective-permute-done.1.refs_2_), slice={[0:544], [0:256]} | slice | bytes 557056 | tf_op jit(solution)/shard_map/slice | solution.py:660
  36.8 0.0 collective-permute-done.4.far
  36.8 3.6 %collective-permute-start.6 = (bf16[544,256]{1,0:T(8,128)(2,1)S(1)}, bf16[544,256]{1,0:T(8,128)(2,1)}, u32[]{:S(2)}, u32[]{:S(2)}) collective-permute-start(bf16[544,256]{1,0:T(8,128)(2,1)S(1)} %slice.3), channel_id=1, source_target_pairs={{0,8},{1,25},{4,12},{5,29},{8,16},{9,1},{12,20},{13,5},{16,24},{17... | collective-permute-start | bytes 835592 | tf_op jit(solution)/shard_map/ppermute | solution.py:634
  40.4 11.8 %near.1 = (bf16[2048,128]{1,0:T(8,128)(2,1)}, f32[2048,128]{1,0:T(8,128)}, f32[2048,128]{1,0:T(8,128)}) custom-call(s32[8]{0:T(128)} %slabs.5, bf16[256,512]{1,0:T(8,128)(2,1)} %get-tuple-element.67.near, bf16[256,512]{1,0:T(8,128)(2,1)} %collective-permute-done.4.far, bf16[8,64,256]{2,1,0:T(8,128)(2,1)} %get-tuple-element.70.notes, ...), custom_call_target="tpu_custom_call" | custom-call | flops 1 | bytes 1 | tf_op jit(solution)/shard_map/near/pallas_call | solution.py:425
  52.3 0.0 collective-permute-done.6.refs_5_
  52.3 10.5 %far.1 = (bf16[2,272,256]{2,1,0:T(8,128)(2,1)}, bf16[272,256]{1,0:T(8,128)(2,1)}, bf16[272,256]{1,0:T(8,128)(2,1)}) custom-call(s32[8]{0:T(128)} %slabs.5, bf16[2048,128]{1,0:T(8,128)(2,1)} %get-tuple-element.71.refs_0_, f32[2048,128]{1,0:T(8,128)} %get-tuple-element.72.refs_1_, f32[2048,128]{1,0:T(8,128)} %get-tuple-element.73.refs_2_, ...), custom_call_target="tpu_custom_call" | custom-call | flops 1073741824 | bytes 262144 | tf_op jit(solution)/shard_map/far/pallas_call | solution.py:509
  62.8 1.3 %collective-permute-start.7 = (bf16[272,256]{1,0:T(8,128)(2,1)}, bf16[272,256]{1,0:T(8,128)(2,1)}, u32[]{:S(2)}, u32[]{:S(2)}) collective-permute-start(bf16[272,256]{1,0:T(8,128)(2,1)} %get-tuple-element.76), channel_id=1, source_target_pairs={{0,2},{2,0},{1,3},{3,1},{4,6},{6,4},{5,7},{7,5},{8,10},{10,8},{9,1... | collective-permute-start | bytes 417800 | tf_op jit(solution)/shard_map/ppermute | solution.py:57
  64.1 0.0 collective-permute-start.8
  64.1 4.0 %all-to-all-start.1 = ((bf16[2,272,256]{2,1,0:T(8,128)(2,1)}), bf16[2,272,256]{2,1,0:T(8,128)(2,1)S(1)}, u32[]{:S(2)}, u32[]{:S(2)}) async-start(bf16[2,272,256]{2,1,0:T(8,128)(2,1)} %get-tuple-element.75), calls=%async_computation.1 | async-start | bytes 557056 | tf_op jit(solution)/shard_map/all_to_all | solution.py:668
  68.1 1.0 %collective-permute-done.10.refs_7_ = bf16[256,2048]{1,0:T(8,128)(2,1)S(1)} collective-permute-done((bf16[256,2048]{1,0:T(8,128)(2,1)}, bf16[256,2048]{1,0:T(8,128)(2,1)S(1)}, u32[]{:S(2)}, u32[]{:S(2)}) %collective-permute-start.10) | collective-permute-done | bytes 1048608 | tf_op jit(solution)/shard_map/ppermute | solution.py:648
  69.1 3.5 %collective-permute-done.9.refs_6_ = bf16[256,2048]{1,0:T(8,128)(2,1)S(1)} collective-permute-done((bf16[256,2048]{1,0:T(8,128)(2,1)}, bf16[256,2048]{1,0:T(8,128)(2,1)S(1)}, u32[]{:S(2)}, u32[]{:S(2)}) %collective-permute-start.9) | collective-permute-done | bytes 1048608 | tf_op jit(solution)/shard_map/ppermute | solution.py:648
  72.6 1.5 %merge.1.refs_0_ = bf16[256,256]{1,0:T(8,128)(2,1)S(1)} custom-call(bf16[2,272,256]{2,1,0:T(8,128)(2,1)S(1)} %all-to-all-done.1.pair, bf16[272,256]{1,0:T(8,128)(2,1)} %collective-permute-done.7.straight, bf16[272,256]{1,0:T(8,128)(2,1)} %collective-permute-done.8.across), custom_call_target="tpu_custom_call" | custom-call | flops 1 | bytes 1 | tf_op jit(solution)/shard_map/merge/pallas_call | solution.py:554
  74.2 2.2 %collective-permute-start.11 = (bf16[256,256]{1,0:T(8,128)(2,1)S(1)}, bf16[256,256]{1,0:T(8,128)(2,1)S(1)}, u32[]{:S(2)}, u32[]{:S(2)}) collective-permute-start(bf16[256,256]{1,0:T(8,128)(2,1)S(1)} %merge.1.refs_0_), channel_id=1, source_target_pairs={{0,64},{32,96},{64,0},{96,32},{1,65},{33,97},{65,1},{97,33},{2,66}... | collective-permute-start | bytes 393224 | tf_op jit(solution)/shard_map/ppermute | solution.py:675
  76.3 0.4 collective-permute-start.12
  76.7 2.3 %collective-permute-start.13 = (bf16[256,256]{1,0:T(8,128)(2,1)S(1)}, bf16[256,256]{1,0:T(8,128)(2,1)S(1)}, u32[]{:S(2)}, u32[]{:S(2)}) collective-permute-start(bf16[256,256]{1,0:T(8,128)(2,1)S(1)} %merge.1.refs_0_), channel_id=1, source_target_pairs={{0,96},{32,0},{64,32},{96,64},{1,97},{33,1},{65,33},{97,65},{2,98}... | collective-permute-start | bytes 393224 | tf_op jit(solution)/shard_map/ppermute | solution.py:675
  79.0 1.4 %collective-permute-done.11.refs_1_ = bf16[256,256]{1,0:T(8,128)(2,1)S(1)} collective-permute-done((bf16[256,256]{1,0:T(8,128)(2,1)S(1)}, bf16[256,256]{1,0:T(8,128)(2,1)S(1)}, u32[]{:S(2)}, u32[]{:S(2)}) %collective-permute-start.11) | collective-permute-done | bytes 131104 | tf_op jit(solution)/shard_map/ppermute | solution.py:675
  80.5 3.2 %collective-permute-done.12.refs_2_ = bf16[256,256]{1,0:T(8,128)(2,1)S(1)} collective-permute-done((bf16[256,256]{1,0:T(8,128)(2,1)S(1)}, bf16[256,256]{1,0:T(8,128)(2,1)S(1)}, u32[]{:S(2)}, u32[]{:S(2)}) %collective-permute-start.12) | collective-permute-done | bytes 131104 | tf_op jit(solution)/shard_map/ppermute | solution.py:675
  83.6 2.5 %project.1 = (bf16[256,1024]{1,0:T(8,128)(2,1)S(1)}, f32[256,1024]{1,0:T(8,128)S(1)}) custom-call(bf16[256,256]{1,0:T(8,128)(2,1)S(1)} %merge.1.refs_0_, bf16[256,256]{1,0:T(8,128)(2,1)S(1)} %collective-permute-done.11.refs_1_, bf16[256,256]{1,0:T(8,128)(2,1)S(1)} %collective-permute-done.12.refs_2_, bf16[256,256]{1,0:T(8,128)(2,1)S(1)} %collective-permute-done.13.refs_3_, ...), custom_call_target="tpu_custom_call" | custom-call | flops 1 | bytes 1 | tf_op jit(solution)/shard_map/project/pallas_call | solution.py:579
  86.1 1.0 collective-permute-start.15
  87.1 1.5 %collective-permute-done.15.got = bf16[256,1024]{1,0:T(8,128)(2,1)S(1)} collective-permute-done((bf16[256,1024]{1,0:T(8,128)(2,1)S(1)}, bf16[256,1024]{1,0:T(8,128)(2,1)S(1)}, u32[]{:S(2)}, u32[]{:S(2)}) %collective-permute-start.15) | collective-permute-done | bytes 524320 | tf_op jit(solution)/shard_map/ppermute | solution.py:57
  88.7 0.1 split.1
  88.8 2.6 %collective-permute-start.16 = (bf16[256,256]{1,0:T(8,128)(2,1)S(1)}, bf16[256,256]{1,0:T(8,128)(2,1)S(1)}, u32[]{:S(2)}, u32[]{:S(2)}) collective-permute-start(bf16[256,256]{1,0:T(8,128)(2,1)S(1)} %get-tuple-element.90), channel_id=1, source_target_pairs={{0,128},{2,130},{128,0},{130,2},{1,129},{3,131},{129,1},{131,3},{4... | collective-permute-start | bytes 393224 | tf_op jit(solution)/shard_map/ppermute | solution.py:680
  91.4 2.7 %collective-permute-start.18 = (bf16[256,256]{1,0:T(8,128)(2,1)S(1)}, bf16[256,256]{1,0:T(8,128)(2,1)S(1)}, u32[]{:S(2)}, u32[]{:S(2)}) collective-permute-start(bf16[256,256]{1,0:T(8,128)(2,1)S(1)} %get-tuple-element.92), channel_id=1, source_target_pairs={{0,130},{2,0},{128,2},{130,128},{1,131},{3,1},{129,3},{131,129},{4... | collective-permute-start | bytes 393224 | tf_op jit(solution)/shard_map/ppermute | solution.py:680
  94.0 1.1 %collective-permute-done.16 = bf16[256,256]{1,0:T(8,128)(2,1)S(1)} collective-permute-done((bf16[256,256]{1,0:T(8,128)(2,1)S(1)}, bf16[256,256]{1,0:T(8,128)(2,1)S(1)}, u32[]{:S(2)}, u32[]{:S(2)}) %collective-permute-start.16) | collective-permute-done | bytes 131104 | tf_op jit(solution)/shard_map/ppermute | solution.py:680
  95.1 3.1 %collective-permute-done.17 = bf16[256,256]{1,0:T(8,128)(2,1)S(1)} collective-permute-done((bf16[256,256]{1,0:T(8,128)(2,1)S(1)}, bf16[256,256]{1,0:T(8,128)(2,1)S(1)}, u32[]{:S(2)}, u32[]{:S(2)}) %collective-permute-start.17) | collective-permute-done | bytes 131104 | tf_op jit(solution)/shard_map/ppermute | solution.py:680
  98.2 0.7 add_convert_fusion
  (17 shorter events, 0.0 us)
Async XLA Ops:
  3.2 22.2 %copy-start.2 = (f32[256,128]{1,0:T(8,128)S(1)}, f32[256,128]{1,0:T(8,128)}, u32[]{:S(2)}) copy-start(f32[256,128]{1,0:T(8,128)} %get-tuple-element.65) | copy-start | bytes 393220
  3.2 22.2 %copy-start.3 = (f32[128]{0:T(128)S(1)}, f32[128]{0:T(128)}, u32[]{:S(2)}) copy-start(f32[128]{0:T(128)} %constant.11) | copy-start | bytes 1540
  3.2 22.2 %copy-start.4 = (f32[128]{0:T(128)S(1)}, f32[128]{0:T(128)}, u32[]{:S(2)}) copy-start(f32[128]{0:T(128)} %constant.12) | copy-start | bytes 1540
  3.2 14.6 %collective-permute-start = (bf16[1088,256]{1,0:T(8,128)(2,1)}, bf16[1088,256]{1,0:T(8,128)(2,1)}, u32[]{:S(2)}, u32[]{:S(2)}) collective-permute-start(bf16[1088,256]{1,0:T(8,128)(2,1)} %get-tuple-element.49.refs_0_), channel_id=1, source_target_pairs={{0,4},{1,29},{4,8},{5,1},{8,12},{9,5},{12,16},{13,9},{16,20},{17,1... | collective-permute-start | bytes 1671176 | tf_op jit(solution)/shard_map/ppermute | solution.py:634
  14.3 5.4 %copy-start.1 = (f32[320,512]{1,0:T(8,128)S(1)}, f32[320,512]{1,0:T(8,128)}, u32[]{:S(2)}) copy-start(f32[320,512]{1,0:T(8,128)} %get-tuple-element.56.keep) | copy-start | bytes 1966084
  14.3 5.4 %collective-permute-start.2 = (bf16[320,512]{1,0:T(8,128)(2,1)}, bf16[320,512]{1,0:T(8,128)(2,1)S(1)}, u32[]{:S(2)}, u32[]{:S(2)}) collective-permute-start(bf16[320,512]{1,0:T(8,128)(2,1)} %get-tuple-element.57), channel_id=1, source_target_pairs={{0,1},{1,0},{2,3},{3,2},{4,5},{5,4},{6,7},{7,6},{8,9},{9,8},{10,11... | collective-permute-start | bytes 983048 | tf_op jit(solution)/shard_map/ppermute | solution.py:57
  17.9 11.5 %collective-permute-start.1 = (bf16[1088,256]{1,0:T(8,128)(2,1)}, bf16[1088,256]{1,0:T(8,128)(2,1)}, u32[]{:S(2)}, u32[]{:S(2)}) collective-permute-start(bf16[1088,256]{1,0:T(8,128)(2,1)} %collective-permute-done.refs_1_), channel_id=1, source_target_pairs={{0,4},{1,29},{4,8},{5,1},{8,12},{9,5},{12,16},{13,9},{16,20},{17,1... | collective-permute-start | bytes 1671176 | tf_op jit(solution)/shard_map/ppermute | solution.py:634
  19.7 8.6 %collective-permute-start.3 = (bf16[288,512]{1,0:T(8,128)(2,1)S(1)}, bf16[288,512]{1,0:T(8,128)(2,1)S(1)}, u32[]{:S(2)}, u32[]{:S(2)}) collective-permute-start(bf16[288,512]{1,0:T(8,128)(2,1)S(1)} %get-tuple-element.64), channel_id=1, source_target_pairs={{0,2},{2,0},{1,3},{3,1},{4,6},{6,4},{5,7},{7,5},{8,10},{10,8},{9,1... | collective-permute-start | bytes 884744 | tf_op jit(solution)/shard_map/ppermute | solution.py:57
  21.0 48.1 %collective-permute-start.10 = (bf16[256,2048]{1,0:T(8,128)(2,1)}, bf16[256,2048]{1,0:T(8,128)(2,1)S(1)}, u32[]{:S(2)}, u32[]{:S(2)}) collective-permute-start(bf16[256,2048]{1,0:T(8,128)(2,1)} %get-tuple-element.79), channel_id=1, source_target_pairs={{0,96},{32,0},{64,32},{96,64},{1,97},{33,1},{65,33},{97,65},{2,98}... | collective-permute-start | bytes 3145736 | tf_op jit(solution)/shard_map/ppermute | solution.py:648
  23.8 48.9 %collective-permute-start.9 = (bf16[256,2048]{1,0:T(8,128)(2,1)}, bf16[256,2048]{1,0:T(8,128)(2,1)S(1)}, u32[]{:S(2)}, u32[]{:S(2)}) collective-permute-start(bf16[256,2048]{1,0:T(8,128)(2,1)} %get-tuple-element.78), channel_id=1, source_target_pairs={{0,32},{32,64},{64,96},{96,0},{1,33},{33,65},{65,97},{97,1},{2,34}... | collective-permute-start | bytes 3145736 | tf_op jit(solution)/shard_map/ppermute | solution.py:648
  23.8 55.3 %collective-permute-start.14 = (bf16[256,2048]{1,0:T(8,128)(2,1)}, bf16[256,2048]{1,0:T(8,128)(2,1)}, u32[]{:S(2)}, u32[]{:S(2)}) collective-permute-start(bf16[256,2048]{1,0:T(8,128)(2,1)} %get-tuple-element.84), channel_id=1, source_target_pairs={{0,64},{32,96},{64,0},{96,32},{1,65},{33,97},{65,1},{97,33},{2,66}... | collective-permute-start | bytes 3145736 | tf_op jit(solution)/shard_map/ppermute | solution.py:648
  29.3 22.9 %collective-permute-start.5 = (bf16[1088,256]{1,0:T(8,128)(2,1)}, bf16[1088,256]{1,0:T(8,128)(2,1)}, u32[]{:S(2)}, u32[]{:S(2)}) collective-permute-start(bf16[1088,256]{1,0:T(8,128)(2,1)} %collective-permute-done.1.refs_2_), channel_id=1, source_target_pairs={{0,4},{1,29},{4,8},{5,1},{8,12},{9,5},{12,16},{13,9},{16,20},{17,1... | collective-permute-start | bytes 1671176 | tf_op jit(solution)/shard_map/ppermute | solution.py:634
  29.5 7.2 %collective-permute-start.4 = (bf16[256,512]{1,0:T(8,128)(2,1)}, bf16[256,512]{1,0:T(8,128)(2,1)}, u32[]{:S(2)}, u32[]{:S(2)}) collective-permute-start(bf16[256,512]{1,0:T(8,128)(2,1)} %get-tuple-element.67.near), channel_id=1, source_target_pairs={{0,1},{1,0},{2,3},{3,2},{4,5},{5,4},{6,7},{7,6},{8,9},{9,8},{10,11... | collective-permute-start | bytes 786440 | tf_op jit(solution)/shard_map/ppermute | solution.py:57
  29.6 22.7 %all-to-all-start = ((bf16[8,64,256]{2,1,0:T(8,128)(2,1)}), bf16[8,64,256]{2,1,0:T(8,128)(2,1)}, u32[]{:S(2)}, u32[]{:S(2)}) async-start(bf16[8,64,256]{2,1,0:T(8,128)(2,1)} %get-tuple-element.70.notes), calls=%async_computation | async-start | bytes 524288 | tf_op jit(solution)/shard_map/all_to_all | solution.py:663
  35.7 47.9 %copy-start = (bf16[256,2048]{1,0:T(8,128)(2,1)S(1)}, bf16[256,2048]{1,0:T(8,128)(2,1)}, u32[]{:S(2)}) copy-start(bf16[256,2048]{1,0:T(8,128)(2,1)} %get-tuple-element.83.refs_4_) | copy-start | bytes 3145732
  36.8 15.5 %collective-permute-start.6 = (bf16[544,256]{1,0:T(8,128)(2,1)S(1)}, bf16[544,256]{1,0:T(8,128)(2,1)}, u32[]{:S(2)}, u32[]{:S(2)}) collective-permute-start(bf16[544,256]{1,0:T(8,128)(2,1)S(1)} %slice.3), channel_id=1, source_target_pairs={{0,8},{1,25},{4,12},{5,29},{8,16},{9,1},{12,20},{13,5},{16,24},{17... | collective-permute-start | bytes 835592 | tf_op jit(solution)/shard_map/ppermute | solution.py:634
  62.8 9.9 %collective-permute-start.7 = (bf16[272,256]{1,0:T(8,128)(2,1)}, bf16[272,256]{1,0:T(8,128)(2,1)}, u32[]{:S(2)}, u32[]{:S(2)}) collective-permute-start(bf16[272,256]{1,0:T(8,128)(2,1)} %get-tuple-element.76), channel_id=1, source_target_pairs={{0,2},{2,0},{1,3},{3,1},{4,6},{6,4},{5,7},{7,5},{8,10},{10,8},{9,1... | collective-permute-start | bytes 417800 | tf_op jit(solution)/shard_map/ppermute | solution.py:57
  64.1 8.6 %collective-permute-start.8 = (bf16[272,256]{1,0:T(8,128)(2,1)}, bf16[272,256]{1,0:T(8,128)(2,1)}, u32[]{:S(2)}, u32[]{:S(2)}) collective-permute-start(bf16[272,256]{1,0:T(8,128)(2,1)} %get-tuple-element.77), channel_id=1, source_target_pairs={{0,3},{1,2},{2,1},{3,0},{4,7},{5,6},{6,5},{7,4},{8,11},{9,10},{10,... | collective-permute-start | bytes 417800 | tf_op jit(solution)/shard_map/ppermute | solution.py:670
  64.1 8.5 %all-to-all-start.1 = ((bf16[2,272,256]{2,1,0:T(8,128)(2,1)}), bf16[2,272,256]{2,1,0:T(8,128)(2,1)S(1)}, u32[]{:S(2)}, u32[]{:S(2)}) async-start(bf16[2,272,256]{2,1,0:T(8,128)(2,1)} %get-tuple-element.75), calls=%async_computation.1 | async-start | bytes 557056 | tf_op jit(solution)/shard_map/all_to_all | solution.py:668
  74.2 6.3 %collective-permute-start.11 = (bf16[256,256]{1,0:T(8,128)(2,1)S(1)}, bf16[256,256]{1,0:T(8,128)(2,1)S(1)}, u32[]{:S(2)}, u32[]{:S(2)}) collective-permute-start(bf16[256,256]{1,0:T(8,128)(2,1)S(1)} %merge.1.refs_0_), channel_id=1, source_target_pairs={{0,64},{32,96},{64,0},{96,32},{1,65},{33,97},{65,1},{97,33},{2,66}... | collective-permute-start | bytes 393224 | tf_op jit(solution)/shard_map/ppermute | solution.py:675
  76.3 7.3 %collective-permute-start.12 = (bf16[256,256]{1,0:T(8,128)(2,1)S(1)}, bf16[256,256]{1,0:T(8,128)(2,1)S(1)}, u32[]{:S(2)}, u32[]{:S(2)}) collective-permute-start(bf16[256,256]{1,0:T(8,128)(2,1)S(1)} %merge.1.refs_0_), channel_id=1, source_target_pairs={{0,32},{32,64},{64,96},{96,0},{1,33},{33,65},{65,97},{97,1},{2,34}... | collective-permute-start | bytes 393224 | tf_op jit(solution)/shard_map/ppermute | solution.py:675
  76.7 6.9 %collective-permute-start.13 = (bf16[256,256]{1,0:T(8,128)(2,1)S(1)}, bf16[256,256]{1,0:T(8,128)(2,1)S(1)}, u32[]{:S(2)}, u32[]{:S(2)}) collective-permute-start(bf16[256,256]{1,0:T(8,128)(2,1)S(1)} %merge.1.refs_0_), channel_id=1, source_target_pairs={{0,96},{32,0},{64,32},{96,64},{1,97},{33,1},{65,33},{97,65},{2,98}... | collective-permute-start | bytes 393224 | tf_op jit(solution)/shard_map/ppermute | solution.py:675
  86.1 2.5 %collective-permute-start.15 = (bf16[256,1024]{1,0:T(8,128)(2,1)S(1)}, bf16[256,1024]{1,0:T(8,128)(2,1)S(1)}, u32[]{:S(2)}, u32[]{:S(2)}) collective-permute-start(bf16[256,1024]{1,0:T(8,128)(2,1)S(1)} %get-tuple-element.88), channel_id=1, source_target_pairs={{0,1},{1,0},{2,3},{3,2},{4,5},{5,4},{6,7},{7,6},{8,9},{9,8},{10,11... | collective-permute-start | bytes 1572872 | tf_op jit(solution)/shard_map/ppermute | solution.py:57
  88.8 6.3 %collective-permute-start.16 = (bf16[256,256]{1,0:T(8,128)(2,1)S(1)}, bf16[256,256]{1,0:T(8,128)(2,1)S(1)}, u32[]{:S(2)}, u32[]{:S(2)}) collective-permute-start(bf16[256,256]{1,0:T(8,128)(2,1)S(1)} %get-tuple-element.90), channel_id=1, source_target_pairs={{0,128},{2,130},{128,0},{130,2},{1,129},{3,131},{129,1},{131,3},{4... | collective-permute-start | bytes 393224 | tf_op jit(solution)/shard_map/ppermute | solution.py:680
  91.4 6.9 %collective-permute-start.17 = (bf16[256,256]{1,0:T(8,128)(2,1)S(1)}, bf16[256,256]{1,0:T(8,128)(2,1)S(1)}, u32[]{:S(2)}, u32[]{:S(2)}) collective-permute-start(bf16[256,256]{1,0:T(8,128)(2,1)S(1)} %get-tuple-element.91), channel_id=1, source_target_pairs={{0,2},{2,128},{128,130},{130,0},{1,3},{3,129},{129,131},{131,1},{4... | collective-permute-start | bytes 393224 | tf_op jit(solution)/shard_map/ppermute | solution.py:680
  91.4 6.9 %collective-permute-start.18 = (bf16[256,256]{1,0:T(8,128)(2,1)S(1)}, bf16[256,256]{1,0:T(8,128)(2,1)S(1)}, u32[]{:S(2)}, u32[]{:S(2)}) collective-permute-start(bf16[256,256]{1,0:T(8,128)(2,1)S(1)} %get-tuple-element.92), channel_id=1, source_target_pairs={{0,130},{2,0},{128,2},{130,128},{1,131},{3,1},{129,3},{131,129},{4... | collective-permute-start | bytes 393224 | tf_op jit(solution)/shard_map/ppermute | solution.py:680

commit v3 on v2

--- a/solution.py
+++ b/solution.py
@@ -669,7 +669,7 @@
         swap(straight, "hid_0"),
         lax.ppermute(across, HID, [(0, 3), (1, 2), (2, 1), (3, 0)]),
     ]
-    parts, weights[2:] = lax.optimization_barrier((parts, weights[2:]))
+    parts, weights[3] = lax.optimization_barrier((parts, weights[3]))
     merged = merge(parts)
 
     heads = [merged] + [lax.ppermute(merged, "head_1", shift(4, by)) for by in (2, 1, 3)]

time: 99.3 us -> 97.9 us (0.986); the launches traced: 98.9 us -> 96.1 us
  Pallas kernels: 38.8 us -> 35.3 us
    pallas_call x1, Pallas kernels: 11.8 us -> 8.39 us  [attend_near(): pl.pallas_call(functools.partial(near_kernel, chunk=chunk, count=count),...]
    ppermute x3, waiting for transfers between devices: 4.5 us -> 2.09 us  [body(): weights.append(lax.ppermute(piece, 'head_1', shift(4, by)))]
    ppermute x4, waiting for transfers between devices: 0.01 us -> 2.37 us  [away(): return lax.ppermute(array, ('key', 'hid_1'), pairs)]
    ppermute x3, waiting for transfers between devices: 4.6 us -> 3.59 us  [body(): lax.ppermute(merged, 'head_1', shift(4, by))]
    ppermute x3, starting transfers between devices: 4.83 us -> 5.84 us  [body(): lax.ppermute(merged, 'head_1', shift(4, by))]
  transfers between devices with their start and end apart: 21 -> 21, of which waited for: 8 -> 8; matrix products, arithmetic and copies ran while one was open for 2% -> 2% of each run, Pallas kernels for 33% -> 31%
where the time goes in v3:
time: 97.9 us; the launch traced here: 96.1 us
  starting transfers between devices  41.4 us (42%)
  Pallas kernels  35.3 us (36%)
  waiting for transfers between devices  16.9 us (17%)
  other arithmetic  1.19 us (1%)
  local copies, waits for them, and re-layouts  1.09 us (1%)
    ppermute x4, starting transfers between devices, away(): return lax.ppermute(array, ('key', 'hid_1'), pairs)  12.1 us
    pallas_call x1, Pallas kernels, attend_far(): pl.pallas_call(functools.partial(far_kernel, chunk=chunk, count=count), o...  10.5 us
    pallas_call x1, Pallas kernels, attend_near(): pl.pallas_call(functools.partial(near_kernel, chunk=chunk, count=count),...  8.39 us
    all_to_all x1, starting transfers between devices, body(): new = lax.all_to_all(notes, 'key', split_axis=0, concat_axis=0, tiled=True)  6.12 us
    ppermute x3, starting transfers between devices, body(): lax.ppermute(merged, 'head_1', shift(4, by))  5.84 us
    ppermute x3, starting transfers between devices, body(): out = out + lax.ppermute(blocks[by - 1], ALONG_X, shift(4, by)).astype(F32)  5.22 us
    all_to_all x1, starting transfers between devices, body(): lax.all_to_all(pair, 'hid_1', split_axis=0, concat_axis=0, tiled=True)  4.93 us
    ppermute x5, waiting for transfers between devices, swap(): return lax.ppermute(array, axis, shift(2, 1))  4.55 us
  transfers between devices with their start and end apart: 21, of which 8 were waited for; matrix products, arithmetic and copies ran while one was open for 2% of the time, Pallas kernels for 31%

profile of v3, /device:TPU:1, one launch (start us, length us, event | category | flops | bytes accessed | tf_op | source)
XLA Modules:
  0.0 96.1 jit_solution(3653989175485826501)
XLA Ops:
  0.0 3.2 %pack.1 = (bf16[1088,256]{1,0:T(8,128)(2,1)}, f32[256,128]{1,0:T(8,128)}) custom-call(s32[8]{0:T(128)} %places.1, s32[8]{0:T(128)} %slabs.5, bf16[2048,128]{1,0:T(8,128)(2,1)} %bitcast.2, bf16[2048,128]{1,0:T(8,128)(2,1)} %bitcast.3), custom_call_target="tpu_custom_call" | custom-call | flops 1 | bytes 1 | tf_op jit(solution)/shard_map/pack/pallas_call | solution.py:101
  3.2 0.0 copy-start.2
  3.2 0.0 copy-start.3
  3.2 0.0 copy-start.4
  3.2 6.5 %collective-permute-start = (bf16[1088,256]{1,0:T(8,128)(2,1)}, bf16[1088,256]{1,0:T(8,128)(2,1)}, u32[]{:S(2)}, u32[]{:S(2)}) collective-permute-start(bf16[1088,256]{1,0:T(8,128)(2,1)} %get-tuple-element.48.refs_0_), channel_id=1, source_target_pairs={{0,4},{1,29},{4,8},{5,1},{8,12},{9,5},{12,16},{13,9},{16,20},{17,1... | collective-permute-start | bytes 1671176 | tf_op jit(solution)/shard_map/ppermute | solution.py:634
  9.7 4.5 %first.1 = (bf16[320,512]{1,0:T(8,128)(2,1)}, f32[320,512]{1,0:T(8,128)}) custom-call(bf16[256,2048]{1,0:T(8,128)(2,1)} %tokens.1, bf16[2048,1024]{1,0:T(8,128)(2,1)} %query.1, bf16[2048,128]{1,0:T(8,128)(2,1)} %key.1, bf16[2048,128]{1,0:T(8,128)(2,1)} %value.1), custom_call_target="tpu_custom_call" | custom-call | flops 1 | bytes 1 | tf_op jit(solution)/shard_map/first/pallas_call | solution.py:192
  14.3 0.1 collective-permute-start.2
  14.4 3.5 %columns.1 = (bf16[256,2048]{1,0:T(8,128)(2,1)}, bf16[256,2048]{1,0:T(8,128)(2,1)}, bf16[256,2048]{1,0:T(8,128)(2,1)}, bf16[256,2048]{1,0:T(8,128)(2,1)}) custom-call(bf16[256,8192]{1,0:T(8,128)(2,1)} %weight.1), custom_call_target="tpu_custom_call" | custom-call | flops 1 | bytes 1 | tf_op jit(solution)/shard_map/columns/pallas_call | solution.py:133
  17.9 0.0 collective-permute-done.refs_1_
  17.9 1.8 %collective-permute-start.1 = (bf16[1088,256]{1,0:T(8,128)(2,1)}, bf16[1088,256]{1,0:T(8,128)(2,1)}, u32[]{:S(2)}, u32[]{:S(2)}) collective-permute-start(bf16[1088,256]{1,0:T(8,128)(2,1)} %collective-permute-done.refs_1_), channel_id=1, source_target_pairs={{0,4},{1,29},{4,8},{5,1},{8,12},{9,5},{12,16},{13,9},{16,20},{17,1... | collective-permute-start | bytes 1671176 | tf_op jit(solution)/shard_map/ppermute | solution.py:634
  19.6 0.1 second.1
  19.7 1.3 %collective-permute-start.3 = (bf16[288,512]{1,0:T(8,128)(2,1)S(1)}, bf16[288,512]{1,0:T(8,128)(2,1)S(1)}, u32[]{:S(2)}, u32[]{:S(2)}) collective-permute-start(bf16[288,512]{1,0:T(8,128)(2,1)S(1)} %get-tuple-element.63), channel_id=1, source_target_pairs={{0,2},{2,0},{1,3},{3,1},{4,6},{6,4},{5,7},{7,5},{8,10},{10,8},{9,1... | collective-permute-start | bytes 884744 | tf_op jit(solution)/shard_map/ppermute | solution.py:57
  21.0 2.7 %collective-permute-start.9 = (bf16[256,2048]{1,0:T(8,128)(2,1)}, bf16[256,2048]{1,0:T(8,128)(2,1)S(1)}, u32[]{:S(2)}, u32[]{:S(2)}) collective-permute-start(bf16[256,2048]{1,0:T(8,128)(2,1)} %get-tuple-element.77), channel_id=1, source_target_pairs={{0,96},{32,0},{64,32},{96,64},{1,97},{33,1},{65,33},{97,65},{2,98}... | collective-permute-start | bytes 3145736 | tf_op jit(solution)/shard_map/ppermute | solution.py:648
  23.8 0.3 collective-permute-start.13
  24.1 0.7 collective-permute-start.14
  24.8 0.5 sine_multiply_fusion
  25.3 3.0 %collective-permute-done.3.got = bf16[288,512]{1,0:T(8,128)(2,1)S(1)} collective-permute-done((bf16[288,512]{1,0:T(8,128)(2,1)S(1)}, bf16[288,512]{1,0:T(8,128)(2,1)S(1)}, u32[]{:S(2)}, u32[]{:S(2)}) %collective-permute-start.3) | collective-permute-done | bytes 294944 | tf_op jit(solution)/shard_map/ppermute | solution.py:57
  28.3 1.0 %rotated.1 = (bf16[256,512]{1,0:T(8,128)(2,1)}, bf16[8,64,256]{2,1,0:T(8,128)(2,1)}) custom-call(f32[288,512]{1,0:T(8,128)S(1)} %get-tuple-element.62.keep, bf16[288,512]{1,0:T(8,128)(2,1)S(1)} %collective-permute-done.3.got, f32[256,128]{1,0:T(8,128)S(1)} %get-tuple-element.92.cosine, f32[256,128]{1,0:T(8,128)S(1)} %get-tuple-element.91.sine), custom_call_target="tpu_custom_call" | custom-call | flops 1 | bytes 1 | tf_op jit(solution)/shard_map/rotated/pallas_call | solution.py:258
  29.3 0.2 collective-permute-start.5
  29.5 0.0 collective-permute-start.4
  29.6 6.1 %all-to-all-start = ((bf16[8,64,256]{2,1,0:T(8,128)(2,1)}), bf16[8,64,256]{2,1,0:T(8,128)(2,1)}, u32[]{:S(2)}, u32[]{:S(2)}) async-start(bf16[8,64,256]{2,1,0:T(8,128)(2,1)} %get-tuple-element.69.notes), calls=%async_computation | async-start | bytes 524288 | tf_op jit(solution)/shard_map/all_to_all | solution.py:663
  35.7 1.1 %slice.3 = bf16[544,256]{1,0:T(8,128)(2,1)S(1)} slice(bf16[1088,256]{1,0:T(8,128)(2,1)} %collective-permute-done.1.refs_2_), slice={[0:544], [0:256]} | slice | bytes 557056 | tf_op jit(solution)/shard_map/slice | solution.py:660
  36.8 3.6 %collective-permute-start.6 = (bf16[544,256]{1,0:T(8,128)(2,1)S(1)}, bf16[544,256]{1,0:T(8,128)(2,1)}, u32[]{:S(2)}, u32[]{:S(2)}) collective-permute-start(bf16[544,256]{1,0:T(8,128)(2,1)S(1)} %slice.3), channel_id=1, source_target_pairs={{0,8},{1,25},{4,12},{5,29},{8,16},{9,1},{12,20},{13,5},{16,24},{17... | collective-permute-start | bytes 835592 | tf_op jit(solution)/shard_map/ppermute | solution.py:634
  40.4 8.4 %near.1 = (bf16[2048,128]{1,0:T(8,128)(2,1)}, f32[2048,128]{1,0:T(8,128)}, f32[2048,128]{1,0:T(8,128)}) custom-call(s32[8]{0:T(128)} %slabs.5, bf16[256,512]{1,0:T(8,128)(2,1)} %get-tuple-element.66.near, bf16[256,512]{1,0:T(8,128)(2,1)} %collective-permute-done.4.far, bf16[8,64,256]{2,1,0:T(8,128)(2,1)} %get-tuple-element.69.notes, ...), custom_call_target="tpu_custom_call" | custom-call | flops 1 | bytes 1 | tf_op jit(solution)/shard_map/near/pallas_call | solution.py:425
  48.8 0.0 all-to-all-done.refs_3_
  48.8 2.4 %collective-permute-done.6.refs_5_ = bf16[544,256]{1,0:T(8,128)(2,1)} collective-permute-done((bf16[544,256]{1,0:T(8,128)(2,1)S(1)}, bf16[544,256]{1,0:T(8,128)(2,1)}, u32[]{:S(2)}, u32[]{:S(2)}) %collective-permute-start.6) | collective-permute-done | bytes 278560 | tf_op jit(solution)/shard_map/ppermute | solution.py:634
  51.2 10.5 %far.1 = (bf16[2,272,256]{2,1,0:T(8,128)(2,1)}, bf16[272,256]{1,0:T(8,128)(2,1)}, bf16[272,256]{1,0:T(8,128)(2,1)}) custom-call(s32[8]{0:T(128)} %slabs.5, bf16[2048,128]{1,0:T(8,128)(2,1)} %get-tuple-element.70.refs_0_, f32[2048,128]{1,0:T(8,128)} %get-tuple-element.71.refs_1_, f32[2048,128]{1,0:T(8,128)} %get-tuple-element.72.refs_2_, ...), custom_call_target="tpu_custom_call" | custom-call | flops 1073741824 | bytes 262144 | tf_op jit(solution)/shard_map/far/pallas_call | solution.py:509
  61.7 0.1 collective-permute-start.7
  61.8 0.4 collective-permute-start.8
  62.1 4.9 %all-to-all-start.1 = ((bf16[2,272,256]{2,1,0:T(8,128)(2,1)}), bf16[2,272,256]{2,1,0:T(8,128)(2,1)S(1)}, u32[]{:S(2)}, u32[]{:S(2)}) async-start(bf16[2,272,256]{2,1,0:T(8,128)(2,1)} %get-tuple-element.74), calls=%async_computation.1 | async-start | bytes 557056 | tf_op jit(solution)/shard_map/all_to_all | solution.py:668
  67.1 2.1 %collective-permute-done.9.refs_7_ = bf16[256,2048]{1,0:T(8,128)(2,1)S(1)} collective-permute-done((bf16[256,2048]{1,0:T(8,128)(2,1)}, bf16[256,2048]{1,0:T(8,128)(2,1)S(1)}, u32[]{:S(2)}, u32[]{:S(2)}) %collective-permute-start.9) | collective-permute-done | bytes 1048608 | tf_op jit(solution)/shard_map/ppermute | solution.py:648
  69.1 0.0 all-to-all-done.1.pair
  69.2 1.5 %merge.1.refs_0_ = bf16[256,256]{1,0:T(8,128)(2,1)S(1)} custom-call(bf16[2,272,256]{2,1,0:T(8,128)(2,1)S(1)} %all-to-all-done.1.pair, bf16[272,256]{1,0:T(8,128)(2,1)} %collective-permute-done.7.straight, bf16[272,256]{1,0:T(8,128)(2,1)} %collective-permute-done.8.across), custom_call_target="tpu_custom_call" | custom-call | flops 1 | bytes 1 | tf_op jit(solution)/shard_map/merge/pallas_call | solution.py:554
  70.7 3.2 %collective-permute-start.10 = (bf16[256,256]{1,0:T(8,128)(2,1)S(1)}, bf16[256,256]{1,0:T(8,128)(2,1)S(1)}, u32[]{:S(2)}, u32[]{:S(2)}) collective-permute-start(bf16[256,256]{1,0:T(8,128)(2,1)S(1)} %merge.1.refs_0_), channel_id=1, source_target_pairs={{0,64},{32,96},{64,0},{96,32},{1,65},{33,97},{65,1},{97,33},{2,66}... | collective-permute-start | bytes 393224 | tf_op jit(solution)/shard_map/ppermute | solution.py:675
  73.8 0.5 collective-permute-start.11
  74.4 2.2 %collective-permute-start.12 = (bf16[256,256]{1,0:T(8,128)(2,1)S(1)}, bf16[256,256]{1,0:T(8,128)(2,1)S(1)}, u32[]{:S(2)}, u32[]{:S(2)}) collective-permute-start(bf16[256,256]{1,0:T(8,128)(2,1)S(1)} %merge.1.refs_0_), channel_id=1, source_target_pairs={{0,96},{32,0},{64,32},{96,64},{1,97},{33,1},{65,33},{97,65},{2,98}... | collective-permute-start | bytes 393224 | tf_op jit(solution)/shard_map/ppermute | solution.py:675
  76.5 3.6 %collective-permute-done.11.refs_2_ = bf16[256,256]{1,0:T(8,128)(2,1)S(1)} collective-permute-done((bf16[256,256]{1,0:T(8,128)(2,1)S(1)}, bf16[256,256]{1,0:T(8,128)(2,1)S(1)}, u32[]{:S(2)}, u32[]{:S(2)}) %collective-permute-start.11) | collective-permute-done | bytes 131104 | tf_op jit(solution)/shard_map/ppermute | solution.py:675
  80.1 2.5 %project.1 = (bf16[256,1024]{1,0:T(8,128)(2,1)S(1)}, f32[256,1024]{1,0:T(8,128)S(1)}) custom-call(bf16[256,256]{1,0:T(8,128)(2,1)S(1)} %merge.1.refs_0_, bf16[256,256]{1,0:T(8,128)(2,1)S(1)} %collective-permute-done.10.refs_1_, bf16[256,256]{1,0:T(8,128)(2,1)S(1)} %collective-permute-done.11.refs_2_, bf16[256,256]{1,0:T(8,128)(2,1)S(1)} %collective-permute-done.12.refs_3_, ...), custom_call_target="tpu_custom_call" | custom-call | flops 1 | bytes 1 | tf_op jit(solution)/shard_map/project/pallas_call | solution.py:579
  82.7 1.6 %collective-permute-start.15 = (bf16[256,1024]{1,0:T(8,128)(2,1)S(1)}, bf16[256,1024]{1,0:T(8,128)(2,1)S(1)}, u32[]{:S(2)}, u32[]{:S(2)}) collective-permute-start(bf16[256,1024]{1,0:T(8,128)(2,1)S(1)} %get-tuple-element.86), channel_id=1, source_target_pairs={{0,1},{1,0},{2,3},{3,2},{4,5},{5,4},{6,7},{7,6},{8,9},{9,8},{10,11... | collective-permute-start | bytes 1572872 | tf_op jit(solution)/shard_map/ppermute | solution.py:57
  84.2 1.5 %collective-permute-done.15.got = bf16[256,1024]{1,0:T(8,128)(2,1)S(1)} collective-permute-done((bf16[256,1024]{1,0:T(8,128)(2,1)S(1)}, bf16[256,1024]{1,0:T(8,128)(2,1)S(1)}, u32[]{:S(2)}, u32[]{:S(2)}) %collective-permute-start.15) | collective-permute-done | bytes 524320 | tf_op jit(solution)/shard_map/ppermute | solution.py:57
  85.8 0.1 split.1
  85.9 2.5 %collective-permute-start.16 = (bf16[256,256]{1,0:T(8,128)(2,1)S(1)}, bf16[256,256]{1,0:T(8,128)(2,1)S(1)}, u32[]{:S(2)}, u32[]{:S(2)}) collective-permute-start(bf16[256,256]{1,0:T(8,128)(2,1)S(1)} %get-tuple-element.88), channel_id=1, source_target_pairs={{0,128},{2,130},{128,0},{130,2},{1,129},{3,131},{129,1},{131,3},{4... | collective-permute-start | bytes 393224 | tf_op jit(solution)/shard_map/ppermute | solution.py:680
  88.5 0.9 collective-permute-start.17
  89.4 1.8 %collective-permute-start.18 = (bf16[256,256]{1,0:T(8,128)(2,1)S(1)}, bf16[256,256]{1,0:T(8,128)(2,1)S(1)}, u32[]{:S(2)}, u32[]{:S(2)}) collective-permute-start(bf16[256,256]{1,0:T(8,128)(2,1)S(1)} %get-tuple-element.90), channel_id=1, source_target_pairs={{0,130},{2,0},{128,2},{130,128},{1,131},{3,1},{129,3},{131,129},{4... | collective-permute-start | bytes 393224 | tf_op jit(solution)/shard_map/ppermute | solution.py:680
  91.1 1.1 %collective-permute-done.16 = bf16[256,256]{1,0:T(8,128)(2,1)S(1)} collective-permute-done((bf16[256,256]{1,0:T(8,128)(2,1)S(1)}, bf16[256,256]{1,0:T(8,128)(2,1)S(1)}, u32[]{:S(2)}, u32[]{:S(2)}) %collective-permute-start.16) | collective-permute-done | bytes 131104 | tf_op jit(solution)/shard_map/ppermute | solution.py:680
  92.2 3.1 %collective-permute-done.17 = bf16[256,256]{1,0:T(8,128)(2,1)S(1)} collective-permute-done((bf16[256,256]{1,0:T(8,128)(2,1)S(1)}, bf16[256,256]{1,0:T(8,128)(2,1)S(1)}, u32[]{:S(2)}, u32[]{:S(2)}) %collective-permute-start.17) | collective-permute-done | bytes 131104 | tf_op jit(solution)/shard_map/ppermute | solution.py:680
  95.3 0.1 collective-permute-done.18
  95.4 0.7 add_convert_fusion
  (17 shorter events, 0.0 us)
Async XLA Ops:
  3.2 21.6 %copy-start.2 = (f32[256,128]{1,0:T(8,128)S(1)}, f32[256,128]{1,0:T(8,128)}, u32[]{:S(2)}) copy-start(f32[256,128]{1,0:T(8,128)} %get-tuple-element.64) | copy-start | bytes 393220
  3.2 21.6 %copy-start.3 = (f32[128]{0:T(128)S(1)}, f32[128]{0:T(128)}, u32[]{:S(2)}) copy-start(f32[128]{0:T(128)} %constant.11) | copy-start | bytes 1540
  3.2 21.6 %copy-start.4 = (f32[128]{0:T(128)S(1)}, f32[128]{0:T(128)}, u32[]{:S(2)}) copy-start(f32[128]{0:T(128)} %constant.12) | copy-start | bytes 1540
  3.2 14.6 %collective-permute-start = (bf16[1088,256]{1,0:T(8,128)(2,1)}, bf16[1088,256]{1,0:T(8,128)(2,1)}, u32[]{:S(2)}, u32[]{:S(2)}) collective-permute-start(bf16[1088,256]{1,0:T(8,128)(2,1)} %get-tuple-element.48.refs_0_), channel_id=1, source_target_pairs={{0,4},{1,29},{4,8},{5,1},{8,12},{9,5},{12,16},{13,9},{16,20},{17,1... | collective-permute-start | bytes 1671176 | tf_op jit(solution)/shard_map/ppermute | solution.py:634
  14.3 5.4 %copy-start.1 = (f32[320,512]{1,0:T(8,128)S(1)}, f32[320,512]{1,0:T(8,128)}, u32[]{:S(2)}) copy-start(f32[320,512]{1,0:T(8,128)} %get-tuple-element.55.keep) | copy-start | bytes 1966084
  14.3 5.4 %collective-permute-start.2 = (bf16[320,512]{1,0:T(8,128)(2,1)}, bf16[320,512]{1,0:T(8,128)(2,1)S(1)}, u32[]{:S(2)}, u32[]{:S(2)}) collective-permute-start(bf16[320,512]{1,0:T(8,128)(2,1)} %get-tuple-element.56), channel_id=1, source_target_pairs={{0,1},{1,0},{2,3},{3,2},{4,5},{5,4},{6,7},{7,6},{8,9},{9,8},{10,11... | collective-permute-start | bytes 983048 | tf_op jit(solution)/shard_map/ppermute | solution.py:57
  17.9 11.4 %collective-permute-start.1 = (bf16[1088,256]{1,0:T(8,128)(2,1)}, bf16[1088,256]{1,0:T(8,128)(2,1)}, u32[]{:S(2)}, u32[]{:S(2)}) collective-permute-start(bf16[1088,256]{1,0:T(8,128)(2,1)} %collective-permute-done.refs_1_), channel_id=1, source_target_pairs={{0,4},{1,29},{4,8},{5,1},{8,12},{9,5},{12,16},{13,9},{16,20},{17,1... | collective-permute-start | bytes 1671176 | tf_op jit(solution)/shard_map/ppermute | solution.py:634
  19.7 8.6 %collective-permute-start.3 = (bf16[288,512]{1,0:T(8,128)(2,1)S(1)}, bf16[288,512]{1,0:T(8,128)(2,1)S(1)}, u32[]{:S(2)}, u32[]{:S(2)}) collective-permute-start(bf16[288,512]{1,0:T(8,128)(2,1)S(1)} %get-tuple-element.63), channel_id=1, source_target_pairs={{0,2},{2,0},{1,3},{3,1},{4,6},{6,4},{5,7},{7,5},{8,10},{10,8},{9,1... | collective-permute-start | bytes 884744 | tf_op jit(solution)/shard_map/ppermute | solution.py:57
  21.0 48.1 %collective-permute-start.9 = (bf16[256,2048]{1,0:T(8,128)(2,1)}, bf16[256,2048]{1,0:T(8,128)(2,1)S(1)}, u32[]{:S(2)}, u32[]{:S(2)}) collective-permute-start(bf16[256,2048]{1,0:T(8,128)(2,1)} %get-tuple-element.77), channel_id=1, source_target_pairs={{0,96},{32,0},{64,32},{96,64},{1,97},{33,1},{65,33},{97,65},{2,98}... | collective-permute-start | bytes 3145736 | tf_op jit(solution)/shard_map/ppermute | solution.py:648
  23.8 52.8 %collective-permute-start.13 = (bf16[256,2048]{1,0:T(8,128)(2,1)}, bf16[256,2048]{1,0:T(8,128)(2,1)S(1)}, u32[]{:S(2)}, u32[]{:S(2)}) collective-permute-start(bf16[256,2048]{1,0:T(8,128)(2,1)} %get-tuple-element.82), channel_id=1, source_target_pairs={{0,64},{32,96},{64,0},{96,32},{1,65},{33,97},{65,1},{97,33},{2,66}... | collective-permute-start | bytes 3145736 | tf_op jit(solution)/shard_map/ppermute | solution.py:648
  24.1 52.4 %collective-permute-start.14 = (bf16[256,2048]{1,0:T(8,128)(2,1)}, bf16[256,2048]{1,0:T(8,128)(2,1)}, u32[]{:S(2)}, u32[]{:S(2)}) collective-permute-start(bf16[256,2048]{1,0:T(8,128)(2,1)} %get-tuple-element.83), channel_id=1, source_target_pairs={{0,32},{32,64},{64,96},{96,0},{1,33},{33,65},{65,97},{97,1},{2,34}... | collective-permute-start | bytes 3145736 | tf_op jit(solution)/shard_map/ppermute | solution.py:648
  29.3 21.9 %collective-permute-start.5 = (bf16[1088,256]{1,0:T(8,128)(2,1)}, bf16[1088,256]{1,0:T(8,128)(2,1)}, u32[]{:S(2)}, u32[]{:S(2)}) collective-permute-start(bf16[1088,256]{1,0:T(8,128)(2,1)} %collective-permute-done.1.refs_2_), channel_id=1, source_target_pairs={{0,4},{1,29},{4,8},{5,1},{8,12},{9,5},{12,16},{13,9},{16,20},{17,1... | collective-permute-start | bytes 1671176 | tf_op jit(solution)/shard_map/ppermute | solution.py:634
  29.5 7.2 %collective-permute-start.4 = (bf16[256,512]{1,0:T(8,128)(2,1)}, bf16[256,512]{1,0:T(8,128)(2,1)}, u32[]{:S(2)}, u32[]{:S(2)}) collective-permute-start(bf16[256,512]{1,0:T(8,128)(2,1)} %get-tuple-element.66.near), channel_id=1, source_target_pairs={{0,1},{1,0},{2,3},{3,2},{4,5},{5,4},{6,7},{7,6},{8,9},{9,8},{10,11... | collective-permute-start | bytes 786440 | tf_op jit(solution)/shard_map/ppermute | solution.py:57
  29.6 19.3 %all-to-all-start = ((bf16[8,64,256]{2,1,0:T(8,128)(2,1)}), bf16[8,64,256]{2,1,0:T(8,128)(2,1)}, u32[]{:S(2)}, u32[]{:S(2)}) async-start(bf16[8,64,256]{2,1,0:T(8,128)(2,1)} %get-tuple-element.69.notes), calls=%async_computation | async-start | bytes 524288 | tf_op jit(solution)/shard_map/all_to_all | solution.py:663
  35.7 44.4 %copy-start = (bf16[256,2048]{1,0:T(8,128)(2,1)S(1)}, bf16[256,2048]{1,0:T(8,128)(2,1)}, u32[]{:S(2)}) copy-start(bf16[256,2048]{1,0:T(8,128)(2,1)} %get-tuple-element.81.refs_4_) | copy-start | bytes 3145732
  36.8 14.4 %collective-permute-start.6 = (bf16[544,256]{1,0:T(8,128)(2,1)S(1)}, bf16[544,256]{1,0:T(8,128)(2,1)}, u32[]{:S(2)}, u32[]{:S(2)}) collective-permute-start(bf16[544,256]{1,0:T(8,128)(2,1)S(1)} %slice.3), channel_id=1, source_target_pairs={{0,8},{1,25},{4,12},{5,29},{8,16},{9,1},{12,20},{13,5},{16,24},{17... | collective-permute-start | bytes 835592 | tf_op jit(solution)/shard_map/ppermute | solution.py:634
  61.7 7.5 %collective-permute-start.7 = (bf16[272,256]{1,0:T(8,128)(2,1)}, bf16[272,256]{1,0:T(8,128)(2,1)}, u32[]{:S(2)}, u32[]{:S(2)}) collective-permute-start(bf16[272,256]{1,0:T(8,128)(2,1)} %get-tuple-element.75), channel_id=1, source_target_pairs={{0,2},{2,0},{1,3},{3,1},{4,6},{6,4},{5,7},{7,5},{8,10},{10,8},{9,1... | collective-permute-start | bytes 417800 | tf_op jit(solution)/shard_map/ppermute | solution.py:57
  61.8 7.4 %collective-permute-start.8 = (bf16[272,256]{1,0:T(8,128)(2,1)}, bf16[272,256]{1,0:T(8,128)(2,1)}, u32[]{:S(2)}, u32[]{:S(2)}) collective-permute-start(bf16[272,256]{1,0:T(8,128)(2,1)} %get-tuple-element.76), channel_id=1, source_target_pairs={{0,3},{1,2},{2,1},{3,0},{4,7},{5,6},{6,5},{7,4},{8,11},{9,10},{10,... | collective-permute-start | bytes 417800 | tf_op jit(solution)/shard_map/ppermute | solution.py:670
  62.1 7.0 %all-to-all-start.1 = ((bf16[2,272,256]{2,1,0:T(8,128)(2,1)}), bf16[2,272,256]{2,1,0:T(8,128)(2,1)S(1)}, u32[]{:S(2)}, u32[]{:S(2)}) async-start(bf16[2,272,256]{2,1,0:T(8,128)(2,1)} %get-tuple-element.74), calls=%async_computation.1 | async-start | bytes 557056 | tf_op jit(solution)/shard_map/all_to_all | solution.py:668
  70.7 5.8 %collective-permute-start.10 = (bf16[256,256]{1,0:T(8,128)(2,1)S(1)}, bf16[256,256]{1,0:T(8,128)(2,1)S(1)}, u32[]{:S(2)}, u32[]{:S(2)}) collective-permute-start(bf16[256,256]{1,0:T(8,128)(2,1)S(1)} %merge.1.refs_0_), channel_id=1, source_target_pairs={{0,64},{32,96},{64,0},{96,32},{1,65},{33,97},{65,1},{97,33},{2,66}... | collective-permute-start | bytes 393224 | tf_op jit(solution)/shard_map/ppermute | solution.py:675
  73.8 6.3 %collective-permute-start.11 = (bf16[256,256]{1,0:T(8,128)(2,1)S(1)}, bf16[256,256]{1,0:T(8,128)(2,1)S(1)}, u32[]{:S(2)}, u32[]{:S(2)}) collective-permute-start(bf16[256,256]{1,0:T(8,128)(2,1)S(1)} %merge.1.refs_0_), channel_id=1, source_target_pairs={{0,32},{32,64},{64,96},{96,0},{1,33},{33,65},{65,97},{97,1},{2,34}... | collective-permute-start | bytes 393224 | tf_op jit(solution)/shard_map/ppermute | solution.py:675
  74.4 5.8 %collective-permute-start.12 = (bf16[256,256]{1,0:T(8,128)(2,1)S(1)}, bf16[256,256]{1,0:T(8,128)(2,1)S(1)}, u32[]{:S(2)}, u32[]{:S(2)}) collective-permute-start(bf16[256,256]{1,0:T(8,128)(2,1)S(1)} %merge.1.refs_0_), channel_id=1, source_target_pairs={{0,96},{32,0},{64,32},{96,64},{1,97},{33,1},{65,33},{97,65},{2,98}... | collective-permute-start | bytes 393224 | tf_op jit(solution)/shard_map/ppermute | solution.py:675
  82.7 3.1 %collective-permute-start.15 = (bf16[256,1024]{1,0:T(8,128)(2,1)S(1)}, bf16[256,1024]{1,0:T(8,128)(2,1)S(1)}, u32[]{:S(2)}, u32[]{:S(2)}) collective-permute-start(bf16[256,1024]{1,0:T(8,128)(2,1)S(1)} %get-tuple-element.86), channel_id=1, source_target_pairs={{0,1},{1,0},{2,3},{3,2},{4,5},{5,4},{6,7},{7,6},{8,9},{9,8},{10,11... | collective-permute-start | bytes 1572872 | tf_op jit(solution)/shard_map/ppermute | solution.py:57
  85.9 6.3 %collective-permute-start.16 = (bf16[256,256]{1,0:T(8,128)(2,1)S(1)}, bf16[256,256]{1,0:T(8,128)(2,1)S(1)}, u32[]{:S(2)}, u32[]{:S(2)}) collective-permute-start(bf16[256,256]{1,0:T(8,128)(2,1)S(1)} %get-tuple-element.88), channel_id=1, source_target_pairs={{0,128},{2,130},{128,0},{130,2},{1,129},{3,131},{129,1},{131,3},{4... | collective-permute-start | bytes 393224 | tf_op jit(solution)/shard_map/ppermute | solution.py:680
  88.5 6.9 %collective-permute-start.17 = (bf16[256,256]{1,0:T(8,128)(2,1)S(1)}, bf16[256,256]{1,0:T(8,128)(2,1)S(1)}, u32[]{:S(2)}, u32[]{:S(2)}) collective-permute-start(bf16[256,256]{1,0:T(8,128)(2,1)S(1)} %get-tuple-element.89), channel_id=1, source_target_pairs={{0,2},{2,128},{128,130},{130,0},{1,3},{3,129},{129,131},{131,1},{4... | collective-permute-start | bytes 393224 | tf_op jit(solution)/shard_map/ppermute | solution.py:680
  89.4 6.1 %collective-permute-start.18 = (bf16[256,256]{1,0:T(8,128)(2,1)S(1)}, bf16[256,256]{1,0:T(8,128)(2,1)S(1)}, u32[]{:S(2)}, u32[]{:S(2)}) collective-permute-start(bf16[256,256]{1,0:T(8,128)(2,1)S(1)} %get-tuple-element.90), channel_id=1, source_target_pairs={{0,130},{2,0},{128,2},{130,128},{1,131},{3,1},{129,3},{131,129},{4... | collective-permute-start | bytes 393224 | tf_op jit(solution)/shard_map/ppermute | solution.py:680
